TPU v7x, 512 devices: a whole 4x4x16 slice. The times are simulated.
512 devices in a mesh: facet: 128 (over z, y, core), chan: 4 (over x).
Axes of the slice: x: 4, y: 4, z: 16, core: 2. Of those that a mesh axis runs over, the one named last changes fastest.
Arguments:
- taylor: float32 [128, 4, 4, 8192], P('facet', 'chan'), may hold values from -6 to 6
- chan_coord: float32 [4], replicated, may hold values from -1 to 1
- sub_offset: int32 [64, 2], replicated, may hold values from 0 to 65535
- sub_owner: int32 [64], replicated, may hold values from 0 to 127, as said below
- tile_list: int32 [2048], P('facet'), may hold values from -1 to 127, as said below
- fourier: float32 [2048, 4, 64, 256], P('facet', 'chan'), may hold values from -0.5 to 0.5
Outputs:
- visibilities: float32 [2048, 4, 256], P('facet', 'chan')
Inputs may be any that keep to these rules, and one draw needn't show every extreme that they name: `sub_owner`: every position along `facet` owns at most 2 of the listed subgrids, at least one owns exactly 2, and some own none. `tile_list`: on position i along `facet` every entry is -1 where i owns no subgrid, else lies in 0 .. 64 times the number of subgrids i owns, minus one.
All inputs are finite; a program needn't handle non-finite values.
Results may differ from a plain program's by a relative error of at most 0.0003.
Values sent between devices are 32-bit elements; how exact they have to be, the bound alone decides.
A program may use at most 64 MiB of HBM per device.

v0:
```python
import math

import jax
import jax.numpy as jnp
from jax import lax
from jax.sharding import PartitionSpec as P

FACET = 8192
SIDE = 8
SKY = 65536
WIN = 64
TAYLOR = 4
CAP = 2


precise = lax.Precision.HIGHEST


def phase_index(left_side, right_side, period):
    low_part = left_side % 256
    high_part = left_side // 256
    wrapped = (low_part * right_side + high_part * right_side % 256 * 256) % 65536
    return wrapped % period


def turn_angle(index_values, period):
    return 2.0 * math.pi / period * index_values.astype(jnp.float32)


def taylor_powers(chan_coord, order_count):
    columns = [jnp.ones_like(chan_coord)]
    for degree in range(1, order_count):
        columns.append(columns[-1] * chan_coord)
    return jnp.stack(columns, axis=1)


def inverse_window(window, length):
    indices = jnp.arange(length, dtype=jnp.int32)
    angles = turn_angle(indices[:, None] * indices[None, :] % length, length)
    cosines = jnp.cos(angles)
    sines = jnp.sin(angles)
    real_in = window[..., :length]
    imag_in = window[..., length:]
    real_mid = jnp.einsum("...vu,uw->...vw", real_in, cosines, precision=precise) - jnp.einsum(
        "...vu,uw->...vw", imag_in, sines, precision=precise
    )
    imag_mid = jnp.einsum("...vu,uw->...vw", real_in, sines, precision=precise) + jnp.einsum(
        "...vu,uw->...vw", imag_in, cosines, precision=precise
    )
    real_out = jnp.einsum("...vw,vy->...yw", real_mid, cosines, precision=precise) - jnp.einsum(
        "...vw,vy->...yw", imag_mid, sines, precision=precise
    )
    imag_out = jnp.einsum("...vw,vy->...yw", real_mid, sines, precision=precise) + jnp.einsum(
        "...vw,vy->...yw", imag_mid, cosines, precision=precise
    )
    return jnp.concatenate([real_out, imag_out], axis=-1) / length


def slot_ranks(sub_owner):
    positions = jnp.arange(sub_owner.shape[0], dtype=jnp.int32)
    earlier = positions[None, :] < positions[:, None]
    same_owner = sub_owner[None, :] == sub_owner[:, None]
    return jnp.sum((earlier & same_owner).astype(jnp.int32), axis=1)


def facet_windows(channel_image, offsets, anchor_x, anchor_y):
    row_count, facet_width = channel_image.shape
    column_blocks = facet_width // WIN
    folded = (
        channel_image.reshape(row_count, column_blocks, WIN)
        .transpose(0, 2, 1)
        .reshape(row_count * WIN, column_blocks)
    )
    subgrids = offsets.shape[0]
    group_size = math.gcd(subgrids, 8)
    grouped = offsets.reshape(subgrids // group_size, group_size, 2)
    freq_steps = jnp.arange(WIN, dtype=jnp.int32)
    block_starts = WIN * jnp.arange(column_blocks, dtype=jnp.int32)
    inner_pos = anchor_x + freq_steps
    row_pos = anchor_y + jnp.arange(row_count, dtype=jnp.int32)
    factor = float((facet_width * row_count) ** (-0.5))
    group_width = group_size * WIN

    def one_group(offset_pairs):
        column_freq = ((offset_pairs[:, 0:1] + freq_steps[None, :]) % SKY).reshape(group_width)
        coarse_angle = turn_angle(
            phase_index(block_starts[:, None], column_freq[None, :], SKY), SKY
        )
        lookup = jnp.concatenate([jnp.cos(coarse_angle), -jnp.sin(coarse_angle)], axis=1)
        partial_value = jnp.dot(folded, lookup, precision=precise).reshape(
            row_count, WIN, 2 * group_width
        )
        fine_angle = turn_angle(phase_index(inner_pos[:, None], column_freq[None, :], SKY), SKY)
        cos_fine = jnp.cos(fine_angle)
        sin_fine = jnp.sin(fine_angle)
        real_part = partial_value[..., :group_width]
        imag_part = partial_value[..., group_width:]
        real_x = jnp.sum(real_part * cos_fine + imag_part * sin_fine, axis=1).reshape(
            row_count, group_size, WIN
        )
        imag_x = jnp.sum(imag_part * cos_fine - real_part * sin_fine, axis=1).reshape(
            row_count, group_size, WIN
        )
        row_freq = (offset_pairs[:, 1:2] + freq_steps[None, :]) % SKY
        vertical = turn_angle(phase_index(row_pos[None, None, :], row_freq[:, :, None], SKY), SKY)
        cos_v = jnp.cos(vertical)
        sin_v = jnp.sin(vertical)
        real_w = jnp.einsum("gvr,rgu->gvu", cos_v, real_x, precision=precise) + jnp.einsum(
            "gvr,rgu->gvu", sin_v, imag_x, precision=precise
        )
        imag_w = jnp.einsum("gvr,rgu->gvu", cos_v, imag_x, precision=precise) - jnp.einsum(
            "gvr,rgu->gvu", sin_v, real_x, precision=precise
        )
        return jnp.concatenate([real_w, imag_w], axis=-1) * factor

    return lax.map(one_group, grouped).reshape(subgrids, WIN, 2 * WIN)


def add_sources(received):
    return jnp.sum(received, axis=0)


def local(taylor, chan_coord, sub_offset, sub_owner, tile_list, fourier):
    band_count = lax.axis_size("facet")
    band_index = lax.axis_index("facet")
    chan_index = lax.axis_index("chan")
    row_count = taylor.shape[2]
    powers = taylor_powers(chan_coord, TAYLOR)
    chan_steps = jnp.arange(powers.shape[0], dtype=jnp.int32)
    facet_ids = band_index % (SIDE * SIDE)
    anchor_x = facet_ids % SIDE * FACET
    anchor_y = facet_ids // SIDE * FACET + band_index // (SIDE * SIDE) * row_count
    own_row = jnp.sum(jnp.where((chan_steps == chan_index)[:, None], powers, 0.0), axis=0)
    all_terms = lax.all_gather(taylor, "chan", axis=1, tiled=True)
    channel_image = jnp.einsum("t,trx->rx", own_row, all_terms[0], precision=precise)
    windows = facet_windows(channel_image, sub_offset, anchor_x, anchor_y)
    subgrids = windows.shape[0]
    ranks = slot_ranks(sub_owner)
    flat_windows = windows.reshape(subgrids, 2 * WIN * WIN)
    target = sub_owner * CAP + ranks
    outgoing = (
        jnp.zeros((band_count * CAP, 2 * WIN * WIN), jnp.float32).at[target].set(flat_windows)
    )
    owned = add_sources(
        lax.all_to_all(
            outgoing.reshape(band_count, CAP, 2 * WIN * WIN),
            "facet",
            split_axis=0,
            concat_axis=0,
            tiled=True,
        )
    )
    owned = owned * float(band_count ** (-0.5))
    pictures = inverse_window(owned.reshape(CAP, WIN, 2 * WIN), WIN).reshape(CAP * WIN, 2 * WIN)
    usable = tile_list >= 0
    tile_rows = jnp.take(pictures, jnp.maximum(tile_list, 0), axis=0)
    tile_rows = jnp.where(usable[:, None], tile_rows, 0.0)
    blocks = fourier[:, 0]
    vis_count = blocks.shape[2] // 2
    real_t = tile_rows[:, :WIN]
    imag_t = tile_rows[:, WIN:]
    real_f = blocks[..., :vis_count]
    imag_f = blocks[..., vis_count:]
    real_v = jnp.einsum("by,byz->bz", real_t, real_f, precision=precise) - jnp.einsum(
        "by,byz->bz", imag_t, imag_f, precision=precise
    )
    imag_v = jnp.einsum("by,byz->bz", real_t, imag_f, precision=precise) + jnp.einsum(
        "by,byz->bz", imag_t, real_f, precision=precise
    )
    return jnp.concatenate([real_v, imag_v], axis=-1)[:, None, :]


def solution(mesh):
    return jax.shard_map(
        local,
        mesh=mesh,
        in_specs=(
            P("facet", "chan", None, None),
            P(),
            P(),
            P(),
            P("facet"),
            P("facet", "chan", None, None),
        ),
        out_specs=P("facet", "chan", None),
        check_vma=False,
    )
```

profile of v0, /device:TPU:1, one launch (start us, length us, event | category | flops | bytes accessed | tf_op | source)
XLA Modules:
  0.0 493.8 jit_solution(6937675604330063461)
XLA Ops:
  0.7 11.3 %all_gather.3 = f32[1,4,4,8192]{3,2,0,1:T(4,128)S(1)} all-gather(f32[1,1,4,8192]{3,2,0,1:T(4,128)} %bitcast.163), channel_id=1, replica_groups=mesh['facet'=128,'chan'=4] {'chan'}, dimensions={1}, use_global_device_ids=true | all-gather | bytes 655360 | tf_op jit(solution)/shard_map/all_gather | solution.py:134
  13.2 1.0 fusion.152
  14.2 61.7 %while.17 = (s32[]{:T(128)}, f32[8,8,64,128]{3,2,1,0:T(8,128)}, s32[8,8,2]{1,0,2:T(8,128)S(1)}, f32[256,128]{1,0:T(8,128)S(1)}, s32[]{:T(128)}, /*index=5*/s32[]{:T(128)}, s32[]{:T(128)}) while((s32[]{:T(128)}, f32[8,8,64,128]{3,2,1,0:T(8,128)}, s32[8,8,2]{1,0,2:T(8,128)S(1)}, f32[256,128]{1,0:T(8,128)S(1)}, ...), condition=%wide.region_5.6_spmd.clone.clone.clone, body=%wide.region_2.5_spmd.clone.clone.clone.sunk | while | flops 414553248 | bytes 5222457 | solution.py:116
  14.4 1.3 fusion.229
  15.7 1.0 fusion.230
  17.8 0.8 fusion.236
  18.6 0.8 fusion.237
  19.4 0.8 fusion.234
  20.2 0.8 fusion.235
  21.1 0.9 fusion.238
  22.1 1.3 fusion.229
  23.5 1.0 fusion.230
  25.5 0.8 fusion.236
  26.4 0.8 fusion.237
  27.2 0.8 fusion.234
  28.0 0.8 fusion.235
  28.8 0.9 fusion.238
  29.8 1.3 fusion.229
  31.2 1.0 fusion.230
  33.2 0.8 fusion.236
  34.1 0.8 fusion.237
  34.9 0.8 fusion.234
  35.7 0.8 fusion.235
  36.5 0.9 fusion.238
  37.5 1.3 fusion.229
  38.9 1.0 fusion.230
  40.9 0.8 fusion.236
  41.8 0.8 fusion.237
  42.6 0.8 fusion.234
  43.4 0.8 fusion.235
  44.2 0.9 fusion.238
  45.3 1.3 fusion.229
  46.6 1.0 fusion.230
  48.6 0.8 fusion.236
  49.5 0.8 fusion.237
  50.3 0.8 fusion.234
  51.1 0.8 fusion.235
  51.9 0.8 fusion.238
  53.0 1.3 fusion.229
  54.3 1.0 fusion.230
  56.3 0.8 fusion.236
  57.2 0.8 fusion.237
  58.0 0.8 fusion.234
  58.8 0.8 fusion.235
  59.6 0.8 fusion.238
  60.7 1.3 fusion.229
  62.0 1.0 fusion.230
  64.0 0.8 fusion.236
  64.9 0.8 fusion.237
  65.7 0.8 fusion.234
  66.5 0.8 fusion.235
  67.3 0.9 fusion.238
  68.4 1.3 fusion.229
  69.7 1.0 fusion.230
  71.8 0.8 fusion.236
  72.6 0.8 fusion.237
  73.4 0.8 fusion.234
  74.2 0.8 fusion.235
  75.1 0.8 fusion.238
  76.1 7.7 %scatter_custom_fusion = f32[256,8192]{1,0:T(8,128)} fusion(s32[64]{0:T(128)S(1)} %compare_select_fusion.3, f32[]{:T(128)} %constant.355.clone.1, f32[8,8,64,128]{3,2,1,0:T(8,128)} %get-tuple-element.273), kind=kCustom, calls=%fused_computation.166 | custom fusion | bytes 10485764 | tf_op jit(solution)/shard_map/scatter | solution.py:142
  83.8 10.6 %reshape.547 = f32[128,2,8192]{2,1,0:T(2,128)} reshape(f32[256,8192]{1,0:T(8,128)} %scatter_custom_fusion) | data formatting | bytes 16777216 | tf_op jit(solution)/shard_map/reshape | solution.py:146
  94.4 23.2 %all-to-all-start = ((f32[128,2,8192]{2,1,0:T(2,128)}), f32[128,2,8192]{2,1,0:T(2,128)}, u32[]{:S(2)}, u32[]{:S(2)}) async-start(f32[128,2,8192]{2,1,0:T(2,128)} %reshape.547), calls=%async_computation | async-start | bytes 16777216 | tf_op jit(solution)/shard_map/all_to_all | solution.py:145
  117.6 364.1 %all-to-all-done = f32[128,2,8192]{2,1,0:T(2,128)} async-done(((f32[128,2,8192]{2,1,0:T(2,128)}), f32[128,2,8192]{2,1,0:T(2,128)}, u32[]{:S(2)}, u32[]{:S(2)}) %all-to-all-start) | async-done | bytes 8388640 | tf_op jit(solution)/shard_map/all_to_all | solution.py:145
  481.8 5.7 %reduce_sum.57 = f32[2,8192]{1,0:T(2,128)S(1)} reduce(f32[128,2,8192]{2,1,0:T(2,128)} %all-to-all-done, f32[]{:T(128)} %constant.355.clone.1), dimensions={0}, to_apply=%region_7.8 | reduce | flops 2080768 | bytes 8454148 | tf_op jit(solution)/shard_map/reduce_sum | solution.py:120
  (141 shorter events, 18.5 us)
Async XLA Ops:
  0.0 13.0 %copy-start.2 = (f32[4]{0:T(128)S(1)}, f32[4]{0:T(128)}, u32[]{:S(2)}) copy-start(f32[4]{0:T(128)} %param.9) | copy-start | bytes 52
  0.0 12.9 %copy-start.1 = (s32[64,2]{0,1:T(2,128)S(1)}, s32[64,2]{0,1:T(2,128)}, u32[]{:S(2)}) copy-start(s32[64,2]{0,1:T(2,128)} %param.10) | copy-start | bytes 1540
  14.2 61.7 %copy-start.3 = (s32[64]{0:T(128)S(1)}, s32[64]{0:T(128)}, u32[]{:S(2)}) copy-start(s32[64]{0:T(128)} %param.11) | copy-start | bytes 772
  94.4 23.2 %copy-start.4 = (s32[16]{0:T(128)S(1)}, s32[16]{0:T(128)}, u32[]{:S(2)}) copy-start(s32[16]{0:T(128)} %param.12) | copy-start | bytes 196
  94.4 387.4 %all-to-all-start = ((f32[128,2,8192]{2,1,0:T(2,128)}), f32[128,2,8192]{2,1,0:T(2,128)}, u32[]{:S(2)}, u32[]{:S(2)}) async-start(f32[128,2,8192]{2,1,0:T(2,128)} %reshape.547), calls=%async_computation | async-start | bytes 16777216 | tf_op jit(solution)/shard_map/all_to_all | solution.py:145
  487.4 3.6 copy-start
where the time goes:
time: 498 us; the launch traced here: 494 us
  waiting for transfers between devices  364 us (73%)
  matrix products  39.4 us (8%)
  other arithmetic  32.7 us (7%)
  starting transfers between devices  23.2 us (5%)
  local copies, waits for them, and re-layouts  22.5 us (5%)
  blocking collectives  11.3 us (2%)
    all_to_all x1, waiting for transfers between devices, local(): lax.all_to_all(outgoing.reshape(band_count, CAP, 2 * WIN * WIN), 'facet',...  364 us
    all_to_all x1, starting transfers between devices, local(): lax.all_to_all(outgoing.reshape(band_count, CAP, 2 * WIN * WIN), 'facet',...  23.2 us
    all_gather x1, blocking collectives, local(): all_terms = lax.all_gather(taylor, 'chan', axis=1, tiled=True)  11.3 us
    cos x8, other arithmetic, one_group(): jnp.cos(coarse_angle)  10.7 us
    reshape x1, local copies, waits for them, and re-layouts, local(): outgoing.reshape(band_count, CAP, 2 * WIN * WIN)  10.6 us
  transfers between devices with their start and end apart: 1, of which 1 were waited for; matrix products, arithmetic and copies ran while one was open for 0% of the time, Pallas kernels for 0%

commit v1 on v0

v1 whole, which is shorter than its diff:
```python
import functools
import math

import jax
import jax.numpy as jnp
import numpy as np
from jax import lax
from jax.experimental import pallas as pl
from jax.experimental.pallas import tpu as pltpu
from jax.sharding import PartitionSpec as P

FACET = 8192
SIDE = 8
SKY = 65536
WIN = 64
ROWS = 4
CAP = 2
LOW = 128
HIGH = FACET // LOW
COARSE = SKY // LOW
PARTS = 2 * ROWS
MESH = pl.DeviceIdType.MESH

precise = lax.Precision.HIGHEST


def turns(index, period):
    angle = 2.0 * np.pi * (index % period) / period
    return np.cos(angle), np.sin(angle)


def halves(table):
    high = table.astype(jnp.bfloat16)
    low = (table - high.astype(np.float64)).astype(jnp.bfloat16)
    return high, low


def tables(z_count, band_count):
    high_pos = np.arange(HIGH)
    low_pos = np.arange(LOW)
    coarse = np.arange(COARSE)
    cosines, sines = turns(high_pos[:, None] * coarse[None, :], COARSE)
    high, low = halves(np.concatenate([cosines, -sines], axis=1))
    outer = np.concatenate([high, high, low], axis=0)
    cosines, sines = turns(low_pos[:, None] * coarse[None, :], SKY)
    twiddle = np.concatenate([cosines, -sines], axis=1).astype(np.float32)
    cosines, sines = turns(np.arange(SIDE)[:, None] * coarse[None, :], SIDE)
    anchor = np.concatenate([cosines, -sines], axis=1).astype(np.float32)
    cosines, sines = turns(low_pos[:, None] * low_pos[None, :], LOW)
    full = np.concatenate(
        [
            np.concatenate([cosines, sines], axis=1),
            np.concatenate([-sines, cosines], axis=1),
        ],
        axis=0,
    )
    high, low = halves(full)
    inner = np.concatenate([high, high, low], axis=1)
    column = np.arange(PARTS * z_count)
    z_pos = column % z_count
    row_pos = (z_pos % SIDE) * FACET + (z_pos // SIDE) * ROWS + column // z_count // 2
    steps = np.arange(WIN)
    cosines, sines = turns(steps[:, None] * row_pos[None, :], SKY)
    scale = float((FACET * ROWS * band_count) ** -0.5) / WIN
    rows = scale * np.concatenate(
        [
            np.concatenate([cosines, -sines], axis=1),
            np.concatenate([sines, cosines], axis=1),
        ],
        axis=0,
    )
    cosines, sines = turns(steps[:, None] * steps[None, :], WIN)
    across = np.concatenate([cosines, sines], axis=1)
    across = np.concatenate([across] * CAP, axis=0)
    return (
        outer,
        twiddle,
        anchor,
        inner,
        rows.astype(np.float32),
        across.astype(np.float32),
    )


def kernel(
    z_count,
    x_count,
    half,
    owner,
    offset,
    tiles,
    coord,
    taylor,
    fourier,
    outer,
    twiddle,
    anchor,
    inner,
    rows,
    across,
    out,
    taylor_v,
    fourier_v,
    outer_v,
    twiddle_v,
    anchor_v,
    inner_v,
    rows_v,
    across_v,
    lhs,
    coarse_v,
    fine_v,
    freq,
    sent1,
    got1,
    sent2,
    got2,
    sent3,
    got3,
    sent4,
    got4,
    pick0,
    pick1,
    weights,
    load_sem,
    send1,
    recv1,
    send2,
    recv2,
    send3,
    recv3,
    send4,
    recv4,
):
    band = lax.axis_index("facet")
    x_pos = lax.axis_index("chan")
    z_pos = band // PARTS
    part = band % PARTS
    band_count = z_count * PARTS
    subs = 2 * half
    blocks = tiles.shape[0]

    barrier = pltpu.get_barrier_semaphore()
    peers1 = [(part + step) % PARTS for step in range(1, PARTS)]
    peers2 = [(x_pos + step) % x_count for step in range(1, x_count)]
    peers3 = [(z_pos + step) % z_count for step in range(1, z_count)]
    for peer in peers3:
        pl.semaphore_signal(barrier, inc=1, device_id=(peer * PARTS + part, x_pos), device_id_type=MESH)
    for peer in peers1:
        pl.semaphore_signal(barrier, inc=1, device_id=(z_pos * PARTS + peer, x_pos), device_id_type=MESH)
    for peer in peers2:
        pl.semaphore_signal(barrier, inc=1, device_id=(band, peer), device_id_type=MESH)

    loads = []
    for number, (source, target) in enumerate(
        [
            (taylor.at[0, 0], taylor_v),
            (outer, outer_v),
            (anchor, anchor_v),
            (twiddle, twiddle_v),
            (inner, inner_v),
            (rows, rows_v),
            (across, across_v),
            (fourier.at[:, 0], fourier_v),
        ]
    ):
        load = pltpu.make_async_copy(source, target, load_sem.at[number])
        load.start()
        loads.append(load)

    loads[0].wait()
    for high in range(HIGH):
        freq[0, pl.ds(high, ROWS, stride=HIGH), :] = taylor_v[:, high * LOW : (high + 1) * LOW]
    for row in range(ROWS):
        image = freq[0, row * HIGH : (row + 1) * HIGH, :]
        top = image.astype(jnp.bfloat16).astype(jnp.float32)
        stacked = jnp.concatenate([top, image - top, top], axis=0)
        lhs[row * LOW : (row + 1) * LOW, :] = jnp.transpose(stacked).astype(jnp.bfloat16)

    loads[1].wait()
    loads[2].wait()
    loads[3].wait()
    phase = anchor_v[pl.ds(part, 1), :]
    phase_r = phase[:, :COARSE]
    phase_i = phase[:, COARSE:]

    def turn_block(number, carry):
        place = pl.ds(pl.multiple_of(number * 16, 16), 16)
        real = twiddle_v[place, :COARSE]
        imag = twiddle_v[place, COARSE:]
        twiddle_v[place, :COARSE] = real * phase_r - imag * phase_i
        twiddle_v[place, COARSE:] = real * phase_i + imag * phase_r
        return carry

    lax.fori_loop(0, LOW // 16, turn_block, 0)

    loads[4].wait()
    for row in range(ROWS):
        coarse_v[...] = jnp.dot(
            lhs[row * LOW : (row + 1) * LOW, :], outer_v[...], preferred_element_type=jnp.float32
        )

        def fine_block(number, carry):
            start = pl.multiple_of(number * 16, 16)
            place = pl.ds(start, 16)
            real_c = coarse_v[place, :COARSE]
            imag_c = coarse_v[place, COARSE:]
            real_t = twiddle_v[place, :COARSE]
            imag_t = twiddle_v[place, COARSE:]
            real = real_c * real_t - imag_c * imag_t
            imag = real_c * imag_t + imag_c * real_t
            for shift, value in ((0, real), (LOW, imag)):
                top = value.astype(jnp.bfloat16)
                rest = (value - top.astype(jnp.float32)).astype(jnp.bfloat16)
                fine_v[pl.ds(start + shift, 16), :] = top
                fine_v[pl.ds(start + shift + 2 * LOW, 16), :] = rest
                fine_v[pl.ds(start + shift + 4 * LOW, 16), :] = top
            return carry

        lax.fori_loop(0, LOW // 16, fine_block, 0)
        result = jnp.dot(inner_v[...], fine_v[...], preferred_element_type=jnp.float32)
        for group in range(COARSE // LOW):
            freq[group, row * 2 * LOW : (row + 1) * 2 * LOW, :] = result[:, group * LOW : (group + 1) * LOW]

    lane = lax.broadcasted_iota(jnp.int32, (PARTS, LOW), 1)

    def pick(number, carry):
        found = []
        for side in range(2):
            start = offset[number + side * half, 0]
            shift = start % LOW
            first = start // LOW
            second = (first + 1) % (SKY // LOW)
            left = freq[first % 4, pl.ds(first // 4, PARTS, stride=LOW), :]
            right = freq[second % 4, pl.ds(second // 4, PARTS, stride=LOW), :]
            value = jnp.where(lane >= shift, left, right)
            found.append(pltpu.roll(value, (LOW + WIN * side - shift) % LOW, 1))
        sent1[pl.ds(number, PARTS, stride=half), :] = jnp.where(lane < WIN, found[0], found[1])
        return carry

    lax.fori_loop(0, half, pick, 0)

    pl.semaphore_wait(barrier, len(peers1) + len(peers2) + len(peers3))
    copies1 = []
    for step, peer in enumerate(peers1):
        copy = pltpu.make_async_remote_copy(
            src_ref=sent1.at[pl.ds(pl.multiple_of(peer * half, half), half), :],
            dst_ref=got1.at[step],
            send_sem=send1.at[step],
            recv_sem=recv1.at[step],
            device_id=(z_pos * PARTS + peer, x_pos),
            device_id_type=MESH,
        )
        copy.start()
        copies1.append(copy)

    lanes = lax.broadcasted_iota(jnp.int32, (8, subs), 1)
    plain = jnp.zeros((8, subs), jnp.int32)
    swapped = jnp.zeros((8, subs), jnp.int32)
    freq_v = [jnp.int32(0), jnp.int32(0)]
    seen = jnp.int32(0)
    for sub in range(subs):
        holder = owner[sub]
        plain = jnp.where(lanes == sub, holder, plain)
        swapped = jnp.where(lanes == (sub + half) % subs, holder, swapped)
        own = holder == band
        freq_v[0] = jnp.where(own & (seen == 0), offset[sub, 1], freq_v[0])
        freq_v[1] = jnp.where(own & (seen == 1), offset[sub, 1], freq_v[1])
        seen = seen + own.astype(jnp.int32)
    grid_row = lax.broadcasted_iota(jnp.int32, (subs, subs), 0)
    grid_col = lax.broadcasted_iota(jnp.int32, (subs, subs), 1)
    plain_f = plain[:1].astype(jnp.float32)
    swapped_f = swapped[:1].astype(jnp.float32)
    along = jnp.sum(jnp.where(grid_row == grid_col, plain_f, 0.0), axis=1, keepdims=True)
    place = lax.broadcasted_iota(jnp.int32, (band_count, subs), 0).astype(jnp.float32)
    for target, holders, number, wanted in (
        (pick0, plain_f, grid_col, 0.0),
        (pick1, swapped_f, (grid_col + half) % subs, 1.0),
    ):
        same = jnp.where((along == holders) & (grid_row < number), 1.0, 0.0)
        rank = jnp.sum(same, axis=0, keepdims=True)
        target[...] = jnp.where((place == holders) & (rank == wanted), 1.0, 0.0)

    wide = lax.broadcasted_iota(jnp.int32, (blocks, LOW), 1)
    deep = lax.broadcasted_iota(jnp.int32, (blocks, LOW), 0)
    tile = jnp.zeros((blocks, LOW), jnp.int32)
    for block in range(blocks):
        tile = jnp.where(deep == block, tiles[block], tile)
    clipped = jnp.maximum(tile, 0)
    tile_row = clipped % WIN
    tile_slot = clipped // WIN
    angle = (2.0 * math.pi / WIN) * ((wide % WIN * tile_row) % WIN).astype(jnp.float32)
    angle = jnp.where(wide < WIN, angle, angle - 0.5 * math.pi)
    loads[5].wait()
    sums = jnp.dot(jnp.cos(angle), rows_v[...], precision=precise, preferred_element_type=jnp.float32)
    span = PARTS * z_count
    column = lax.broadcasted_iota(jnp.int32, (blocks, span), 1)
    column_z = column % z_count
    column_part = column // z_count
    row_pos = column_z % SIDE * FACET + column_z // SIDE * ROWS + column_part // 2
    slot_v = jnp.where(tile_slot[:, :1] == 0, freq_v[0], freq_v[1])
    angle = (2.0 * math.pi / SKY) * ((slot_v * row_pos) & (SKY - 1)).astype(jnp.float32)
    cosines = jnp.cos(angle)
    sines = jnp.sin(angle)
    real = sums[:, :span] * cosines + sums[:, span:] * sines
    imag = sums[:, span:] * cosines - sums[:, :span] * sines
    usable = tile[:, :1] >= 0
    real = jnp.where(usable, real, 0.0)
    imag = jnp.where(usable, imag, 0.0)
    even = column_part % 2 == 0
    weights[:blocks, :] = jnp.where(even, real, -imag)
    weights[blocks:, :] = jnp.where(even, imag, real)

    total = sent1[pl.ds(pl.multiple_of(part * half, half), half), :]
    for step, copy in enumerate(copies1):
        copy.wait_recv()
        total = total + got1[step]
    sent2[...] = total

    copies2 = []
    for step, peer in enumerate(peers2):
        copy = pltpu.make_async_remote_copy(
            src_ref=sent2,
            dst_ref=got2.at[step],
            send_sem=send2.at[step],
            recv_sem=recv2.at[step],
            device_id=(band, peer),
            device_id_type=MESH,
        )
        copy.start()
        copies2.append(copy)
    here = coord[x_pos]

    def power(term):
        value = jnp.float32(1.0)
        product = jnp.float32(1.0)
        for degree in range(1, x_count):
            product = product * here
            value = jnp.where(term == degree, product, value)
        return value

    mixed = power(x_pos) * total
    for step, copy in enumerate(copies2):
        copy.wait_recv()
        mixed = mixed + power((x_pos + x_count - step - 1) % x_count) * got2[step]

    pair = jnp.concatenate([mixed, pltpu.roll(mixed, WIN, 1)], axis=0)
    slot0 = jnp.dot(pick0[...], pair, precision=precise, preferred_element_type=jnp.float32)
    slot1 = jnp.dot(pick1[...], pair, precision=precise, preferred_element_type=jnp.float32)
    slot_lane = lax.broadcasted_iota(jnp.int32, (band_count, LOW), 1)
    sent3[...] = jnp.where(slot_lane < WIN, slot0, slot1)
    own_z = pl.ds(pl.multiple_of(z_pos * PARTS, PARTS), PARTS)
    copies3 = []
    for step, peer in enumerate(peers3):
        copy = pltpu.make_async_remote_copy(
            src_ref=sent3.at[pl.ds(pl.multiple_of(peer * PARTS, PARTS), PARTS), :],
            dst_ref=got3.at[own_z, :],
            send_sem=send3.at[step],
            recv_sem=recv3.at[step],
            device_id=(peer * PARTS + part, x_pos),
            device_id_type=MESH,
        )
        copy.start()
        copies3.append(copy)
    got3[own_z, :] = sent3[own_z, :]
    for step in range(1, z_count):
        source = (z_pos + z_count - step) % z_count
        pltpu.make_async_remote_copy(
            src_ref=sent3.at[own_z, :],
            dst_ref=got3.at[pl.ds(pl.multiple_of(source * PARTS, PARTS), PARTS), :],
            send_sem=send3.at[step - 1],
            recv_sem=recv3.at[step - 1],
            device_id=(source * PARTS + part, x_pos),
            device_id_type=MESH,
        ).wait_recv()
    for peer in range(PARTS):
        sent4[peer * z_count : (peer + 1) * z_count, :] = got3[pl.ds(peer, z_count, stride=PARTS), :]
    own_part = pl.ds(pl.multiple_of(part * z_count, z_count), z_count)
    copies4 = []
    for step, peer in enumerate(peers1):
        copy = pltpu.make_async_remote_copy(
            src_ref=sent4.at[pl.ds(pl.multiple_of(peer * z_count, z_count), z_count), :],
            dst_ref=got4.at[own_part, :],
            send_sem=send4.at[step],
            recv_sem=recv4.at[step],
            device_id=(z_pos * PARTS + peer, x_pos),
            device_id_type=MESH,
        )
        copy.start()
        copies4.append(copy)
    got4[own_part, :] = sent4[own_part, :]
    for step in range(1, PARTS):
        source = (part + PARTS - step) % PARTS
        pltpu.make_async_remote_copy(
            src_ref=sent4.at[own_part, :],
            dst_ref=got4.at[pl.ds(pl.multiple_of(source * z_count, z_count), z_count), :],
            send_sem=send4.at[step - 1],
            recv_sem=recv4.at[step - 1],
            device_id=(z_pos * PARTS + source, x_pos),
            device_id_type=MESH,
        ).wait_recv()

    loads[6].wait()
    loads[7].wait()
    lines = jnp.dot(weights[...], got4[...], precision=precise, preferred_element_type=jnp.float32)
    keep = wide // WIN == tile_slot
    lines = jnp.where(jnp.concatenate([keep, keep], axis=0), lines, 0.0)
    spread = jnp.dot(lines, across_v[...], precision=precise, preferred_element_type=jnp.float32)
    crossed = pltpu.roll(spread[blocks:], WIN, 1)
    tile_rows = spread[:blocks] + jnp.where(wide < WIN, -crossed, crossed)
    upright = jnp.transpose(tile_rows)
    for block in range(blocks):
        real_t = upright[:WIN, block : block + 1]
        imag_t = upright[WIN:, block : block + 1]
        real_f = fourier_v[block, :, :LOW]
        imag_f = fourier_v[block, :, LOW:]
        out[block : block + 1, :LOW] = jnp.sum(real_t * real_f - imag_t * imag_f, axis=0, keepdims=True)
        out[block : block + 1, LOW:] = jnp.sum(real_t * imag_f + imag_t * real_f, axis=0, keepdims=True)

    for copy in copies1 + copies2 + copies3 + copies4:
        copy.wait_send()


def local(z_count, x_count, taylor, chan_coord, sub_offset, sub_owner, tile_list, fourier):
    constants = tables(z_count, z_count * PARTS)
    half = sub_owner.shape[0] // 2
    blocks = tile_list.shape[0]
    band_count = z_count * PARTS
    scratch = [
        pltpu.VMEM((ROWS, FACET), jnp.float32),
        pltpu.VMEM((blocks, WIN, 2 * LOW), jnp.float32),
    ]
    scratch += [pltpu.VMEM(table.shape, table.dtype) for table in constants]
    scratch += [
        pltpu.VMEM((ROWS * LOW, 3 * HIGH), jnp.bfloat16),
        pltpu.VMEM((LOW, 2 * COARSE), jnp.float32),
        pltpu.VMEM((6 * LOW, COARSE), jnp.bfloat16),
        pltpu.VMEM((COARSE // LOW, PARTS * LOW, LOW), jnp.float32),
        pltpu.VMEM((PARTS * half, LOW), jnp.float32),
        pltpu.VMEM((PARTS - 1, half, LOW), jnp.float32),
        pltpu.VMEM((half, LOW), jnp.float32),
        pltpu.VMEM((max(x_count - 1, 1), half, LOW), jnp.float32),
        pltpu.VMEM((band_count, LOW), jnp.float32),
        pltpu.VMEM((band_count, LOW), jnp.float32),
        pltpu.VMEM((band_count, LOW), jnp.float32),
        pltpu.VMEM((band_count, LOW), jnp.float32),
        pltpu.VMEM((band_count, 2 * half), jnp.float32),
        pltpu.VMEM((band_count, 2 * half), jnp.float32),
        pltpu.VMEM((2 * blocks, band_count), jnp.float32),
        pltpu.SemaphoreType.DMA((8,)),
    ]
    for count in (PARTS, max(x_count, 2), max(z_count, 2), PARTS):
        scratch += [pltpu.SemaphoreType.DMA((count - 1,))] * 2
    small = pl.BlockSpec(memory_space=pltpu.SMEM)
    large = pl.BlockSpec(memory_space=pl.ANY)
    visibilities = pl.pallas_call(
        functools.partial(kernel, z_count, x_count, half),
        out_shape=jax.ShapeDtypeStruct((blocks, 2 * LOW), jnp.float32),
        in_specs=[small] * 4 + [large] * (2 + len(constants)),
        out_specs=pl.BlockSpec(memory_space=pltpu.VMEM),
        scratch_shapes=scratch,
        compiler_params=pltpu.CompilerParams(collective_id=0, has_side_effects=True),
    )(sub_owner, sub_offset, tile_list, chan_coord, taylor, fourier, *[jnp.asarray(table) for table in constants])
    return visibilities[:, None, :]


def solution(mesh):
    return jax.shard_map(
        functools.partial(local, mesh.shape["facet"] // PARTS, mesh.shape["chan"]),
        mesh=mesh,
        in_specs=(
            P("facet", "chan", None, None),
            P(),
            P(),
            P(),
            P("facet"),
            P("facet", "chan", None, None),
        ),
        out_specs=P("facet", "chan", None),
        check_vma=False,
    )
```

time: 498 us -> 45.7 us (0.09)
  waiting for transfers between devices: 364 us -> 0 us
  Pallas kernels: 0 us -> 42.7 us
  matrix products: 39.4 us -> 0 us
  other arithmetic: 32.7 us -> 0 us
  starting transfers between devices: 23.2 us -> 0 us
  local copies, waits for them, and re-layouts: 22.5 us -> 2.71 us
  blocking collectives: 11.3 us -> 0 us
    all_to_all x1 -> x0, waiting for transfers between devices: 364 us -> none  [local(): lax.all_to_all(outgoing.reshape(band_count, CAP, 2 * WIN * WIN), 'facet',...]
    pallas_call x0 -> x1, Pallas kernels: none -> 42.7 us  [local(): pl.pallas_call(functools.partial(kernel, z_count, x_count, half), out_sha...]
    dot_general x53 -> x0, matrix products: 39.4 us -> none  [the longest x8 8.06 us: one_group(): jnp.dot(folded, lookup, precision=precise)]
    all_to_all x1 -> x0, starting transfers between devices: 23.2 us -> none  [local(): lax.all_to_all(outgoing.reshape(band_count, CAP, 2 * WIN * WIN), 'facet',...]
    cos x16 -> x0, other arithmetic: 16.3 us -> none  [the longest x8 10.7 us: one_group(): jnp.cos(coarse_angle)]
    reshape x18 -> x0, local copies, waits for them, and re-layouts: 11.9 us -> none  [the longest x1 10.6 us: local(): outgoing.reshape(band_count, CAP, 2 * WIN * WIN)]
    all_gather x1 -> x0, blocking collectives: 11.3 us -> none  [local(): all_terms = lax.all_gather(taylor, 'chan', axis=1, tiled=True)]
    scatter x1 -> x0, local copies, waits for them, and re-layouts: 7.71 us -> none  [local(): jnp.zeros((band_count * CAP, 2 * WIN * WIN), jnp.float32).at[target]]
  transfers between devices with their start and end apart: 1 -> 0, of which waited for: 1 -> 0; matrix products, arithmetic and copies ran while one was open for 0% -> 0% of each run, Pallas kernels for 0% -> 0%
where the time goes in v1:
time: 45.7 us; the launch traced here: 45.4 us
  Pallas kernels  42.7 us (93%)
  local copies, waits for them, and re-layouts  2.71 us (6%)
    pallas_call x1, Pallas kernels, local(): pl.pallas_call(functools.partial(kernel, z_count, x_count, half), out_sha...  42.7 us
    unnamed x1, local copies, waits for them, and re-layouts  1.37 us
    broadcast_in_dim x1, local copies, waits for them, and re-layouts, local(): return visibilities[:, None, :]  1.34 us

profile of v1, /device:TPU:1, one launch (start us, length us, event | category | flops | bytes accessed | tf_op | source)
XLA Modules:
  0.0 45.4 jit_solution(12444208805148373453)
XLA Ops:
  0.0 1.4 %copy.13.offset = s32[64,2]{1,0:T(8,128)} copy(s32[64,2]{0,1:T(2,128)} %param.14) | data formatting | bytes 1024 | tf_op args[2]
  1.4 42.7 %shard_map.118 = f32[16,256]{1,0:T(8,128)} custom-call(s32[64]{0:T(128)} %owner.1, s32[64,2]{1,0:T(8,128)} %copy.13.offset, s32[16]{0:T(128)} %tiles.1, f32[4]{0:T(128)} %coord.1, f32[1,1,4,8192]{3,2,1,0:T(4,128)} %taylor.1, f32[16,1,64,256]{3,2,1,0:T(8,128)} %fourier.1, bf16[192,1024]{1,0:T(8,128)(2,1)} %constant.12.clone.outer, ...), custom_call_target="tpu_custom_call" | custom-call | tf_op jit(solution)/shard_map/pallas_call | solution.py:456
  44.1 1.3 %copy.14 = f32[16,1,256]{2,1,0:T(1,128)} copy(f32[16,1,256]{2,0,1:T(8,128)} %bitcast.1) | data formatting | bytes 32768 | tf_op jit(solution)/shard_map/broadcast_in_dim | solution.py:464

commit v2 on v1

v2 whole, which is shorter than its diff:
```python
import functools
import math

import jax
import jax.numpy as jnp
import numpy as np
from jax import lax
from jax.experimental import pallas as pl
from jax.experimental.pallas import tpu as pltpu
from jax.sharding import PartitionSpec as P

FACET = 8192
SIDE = 8
SKY = 65536
WIN = 64
ROWS = 4
CAP = 2
LOW = 128
HIGH = FACET // LOW
COARSE = SKY // LOW
PARTS = 2 * ROWS
MESH = pl.DeviceIdType.MESH

precise = lax.Precision.HIGHEST


def turns(index, period):
    angle = 2.0 * np.pi * (index % period) / period
    return np.cos(angle), np.sin(angle)


def halves(table):
    high = table.astype(jnp.bfloat16)
    low = (table - high.astype(np.float64)).astype(jnp.bfloat16)
    return high, low


def tables(z_count, band_count):
    low_pos = np.arange(LOW)
    coarse = np.arange(COARSE)
    high_pos = np.arange(SIDE * HIGH)
    cosines, sines = turns(high_pos[:, None] * coarse[None, :], COARSE)
    outer = np.stack(halves(np.concatenate([cosines, -sines], axis=1)))
    cosines, sines = turns(low_pos[:, None] * coarse[None, :], SKY)
    twiddle = np.concatenate([cosines, -sines], axis=1).astype(np.float32)
    cosines, sines = turns(low_pos[:, None] * low_pos[None, :], LOW)
    full = np.concatenate(
        [
            np.concatenate([cosines, sines], axis=1),
            np.concatenate([-sines, cosines], axis=1),
        ],
        axis=0,
    )
    inner = np.stack(halves(full))
    column = np.arange(PARTS * z_count)
    z_pos = column // PARTS
    row_pos = (z_pos % SIDE) * FACET + (z_pos // SIDE) * ROWS + column % PARTS // 2
    steps = np.arange(WIN)
    cosines, sines = turns(steps[:, None] * row_pos[None, :], SKY)
    scale = float((FACET * ROWS * band_count) ** -0.5) / WIN
    rows = scale * np.concatenate(
        [
            np.concatenate([cosines, -sines], axis=1),
            np.concatenate([sines, cosines], axis=1),
        ],
        axis=0,
    )
    cosines, sines = turns(steps[:, None] * steps[None, :], WIN)
    across = np.concatenate([cosines, sines], axis=1)
    across = np.concatenate([across] * CAP, axis=0)
    return (
        outer,
        twiddle,
        inner,
        rows.astype(np.float32),
        across.astype(np.float32),
    )


def kernel(
    z_count,
    x_count,
    half,
    owner_h,
    offset_h,
    tiles_h,
    coord_h,
    taylor,
    fourier,
    outer,
    twiddle,
    inner,
    rows,
    across,
    out,
    owner,
    offset,
    tiles,
    coord,
    taylor_v,
    fourier_v,
    outer_v,
    twiddle_v,
    inner_v,
    rows_v,
    across_v,
    lhs,
    coarse_v,
    fine_v,
    freq,
    sent1,
    got1,
    sent2,
    got2,
    sent3,
    got3,
    pick0,
    pick1,
    weights,
    load_sem,
    send1,
    recv1,
    send2,
    recv2,
    send3,
    recv3,
):
    band = lax.axis_index("facet")
    x_pos = lax.axis_index("chan")
    z_pos = band // PARTS
    part = band % PARTS
    band_count = z_count * PARTS
    subs = 2 * half
    blocks = tiles.shape[0]

    loads = []
    for number, (source, target) in enumerate(
        [
            (taylor.at[0, 0], taylor_v),
            (outer.at[0, pl.ds(pl.multiple_of(part * HIGH, HIGH), HIGH), :], outer_v.at[:HIGH, :]),
            (outer.at[0, pl.ds(pl.multiple_of(part * HIGH, HIGH), HIGH), :], outer_v.at[HIGH : 2 * HIGH, :]),
            (outer.at[1, pl.ds(pl.multiple_of(part * HIGH, HIGH), HIGH), :], outer_v.at[2 * HIGH :, :]),
            (twiddle, twiddle_v),
            (inner.at[0], inner_v.at[:, : 2 * LOW]),
            (inner.at[0], inner_v.at[:, 2 * LOW : 4 * LOW]),
            (inner.at[1], inner_v.at[:, 4 * LOW :]),
            (offset_h, offset),
            (owner_h, owner),
            (tiles_h, tiles),
            (coord_h, coord),
            (rows, rows_v),
            (across, across_v),
            (fourier.at[:, 0], fourier_v),
        ]
    ):
        load = pltpu.make_async_copy(source, target, load_sem.at[number])
        load.start()
        loads.append(load)

    def wrapped(place, step, count):
        moved = place + step
        return jnp.where(moved >= count, moved - count, moved)

    barrier = pltpu.get_barrier_semaphore()
    far = sorted(range(z_count), key=lambda step: -min(step, z_count - step))
    peers_x = [wrapped(x_pos, step, x_count) for step in range(1, x_count)]
    parts = [wrapped(part, step, PARTS) for step in range(PARTS)]
    peers1 = [z_pos * PARTS + peer for peer in parts[1:]]
    peers3 = []
    for step in far:
        base = wrapped(z_pos, step, z_count) * PARTS
        peers3 += [base + peer for peer in (parts if step else parts[1:])]
    greeted = [wrapped(z_pos, step, z_count) * PARTS + part for step in far if step] + peers1
    for peer in greeted:
        pl.semaphore_signal(barrier, inc=1, device_id=(peer, x_pos), device_id_type=MESH)
    for peer in peers_x:
        pl.semaphore_signal(barrier, inc=1, device_id=(band, peer), device_id_type=MESH)

    loads[0].wait()
    for high in range(HIGH):
        freq[0, pl.ds(high, ROWS, stride=HIGH), :] = taylor_v[:, high * LOW : (high + 1) * LOW]
    for row in range(ROWS):
        image = freq[0, row * HIGH : (row + 1) * HIGH, :]
        top = image.astype(jnp.bfloat16).astype(jnp.float32)
        stacked = jnp.concatenate([top, image - top, top], axis=0)
        lhs[row * LOW : (row + 1) * LOW, :] = jnp.transpose(stacked).astype(jnp.bfloat16)

    for load in loads[1:8]:
        load.wait()
    for row in range(ROWS):
        coarse_v[row] = jnp.dot(
            lhs[row * LOW : (row + 1) * LOW, :], outer_v[...], preferred_element_type=jnp.float32
        )
        for start in range(0, LOW, 16):
            real_c = coarse_v[row, start : start + 16, :COARSE]
            imag_c = coarse_v[row, start : start + 16, COARSE:]
            real_t = twiddle_v[start : start + 16, :COARSE]
            imag_t = twiddle_v[start : start + 16, COARSE:]
            real = real_c * real_t - imag_c * imag_t
            imag = real_c * imag_t + imag_c * real_t
            for shift, value in ((start, real), (start + LOW, imag)):
                top = value.astype(jnp.bfloat16)
                rest = (value - top.astype(jnp.float32)).astype(jnp.bfloat16)
                fine_v[row, shift : shift + 16, :] = top
                fine_v[row, shift + 2 * LOW : shift + 2 * LOW + 16, :] = rest
                fine_v[row, shift + 4 * LOW : shift + 4 * LOW + 16, :] = top
        result = jnp.dot(inner_v[...], fine_v[row], preferred_element_type=jnp.float32)
        for group in range(COARSE // LOW):
            freq[group, row * 2 * LOW : (row + 1) * 2 * LOW, :] = result[:, group * LOW : (group + 1) * LOW]

    for load in loads[8:12]:
        load.wait()
    lane = lax.broadcasted_iota(jnp.int32, (PARTS, LOW), 1)
    bunch = min(8, half)

    def pick(number, carry):
        found = []
        for place in range(bunch):
            for side in range(2):
                start = offset[0, number * bunch + place + side * half]
                shift = start & (LOW - 1)
                first = lax.shift_right_logical(start, 7)
                second = (first + 1) & (SKY // LOW - 1)
                left = freq[first & 3, pl.ds(lax.shift_right_logical(first, 2), PARTS, stride=LOW), :]
                right = freq[second & 3, pl.ds(lax.shift_right_logical(second, 2), PARTS, stride=LOW), :]
                value = jnp.where(lane >= shift, left, right)
                found.append(pltpu.roll(value, (LOW + WIN * side - shift) & (LOW - 1), 1))
        for place in range(bunch):
            value = jnp.where(lane < WIN, found[2 * place], found[2 * place + 1])
            sent1[pl.ds(number * bunch + place, PARTS, stride=half), :] = value
        return carry

    lax.fori_loop(0, half // bunch, pick, 0)

    pl.semaphore_wait(barrier, len(peers_x) + len(greeted))
    copies1 = []
    for step, peer in enumerate(peers1):
        copy = pltpu.make_async_remote_copy(
            src_ref=sent1.at[pl.ds(pl.multiple_of(parts[step + 1] * half, half), half), :],
            dst_ref=got1.at[step],
            send_sem=send1.at[step],
            recv_sem=recv1.at[step],
            device_id=(peer, x_pos),
            device_id_type=MESH,
        )
        copy.start()
        copies1.append(copy)

    lanes = lax.broadcasted_iota(jnp.int32, (8, subs), 1)
    plain = jnp.zeros((8, subs), jnp.int32)
    swapped = jnp.zeros((8, subs), jnp.int32)
    freq_v = [jnp.int32(0), jnp.int32(0)]
    seen = jnp.int32(0)
    for sub in range(subs):
        holder = owner[sub]
        plain = jnp.where(lanes == sub, holder, plain)
        swapped = jnp.where(lanes == (sub + half) % subs, holder, swapped)
        own = holder == band
        freq_v[0] = jnp.where(own & (seen == 0), offset[1, sub], freq_v[0])
        freq_v[1] = jnp.where(own & (seen == 1), offset[1, sub], freq_v[1])
        seen = seen + own.astype(jnp.int32)
    grid_row = lax.broadcasted_iota(jnp.int32, (subs, subs), 0)
    grid_col = lax.broadcasted_iota(jnp.int32, (subs, subs), 1)
    plain_f = plain[:1].astype(jnp.float32)
    swapped_f = swapped[:1].astype(jnp.float32)
    along = jnp.sum(jnp.where(grid_row == grid_col, plain_f, 0.0), axis=1, keepdims=True)
    place = lax.broadcasted_iota(jnp.int32, (band_count, subs), 0).astype(jnp.float32)
    for target, holders, number, wanted in (
        (pick0, plain_f, grid_col, 0.0),
        (pick1, swapped_f, (grid_col + half) % subs, 1.0),
    ):
        same = jnp.where((along == holders) & (grid_row < number), 1.0, 0.0)
        rank = jnp.sum(same, axis=0, keepdims=True)
        target[...] = jnp.where((place == holders) & (rank == wanted), 1.0, 0.0)

    total = sent1[pl.ds(pl.multiple_of(part * half, half), half), :]
    for step, copy in enumerate(copies1):
        copy.wait_recv()
        total = total + got1[step]
    sent2[...] = total

    copies2 = []
    for step, peer in enumerate(peers_x):
        copy = pltpu.make_async_remote_copy(
            src_ref=sent2,
            dst_ref=got2.at[step],
            send_sem=send2.at[step],
            recv_sem=recv2.at[step],
            device_id=(band, peer),
            device_id_type=MESH,
        )
        copy.start()
        copies2.append(copy)
    here = coord[x_pos]

    def power(term):
        value = jnp.float32(1.0)
        product = jnp.float32(1.0)
        for degree in range(1, x_count):
            product = product * here
            value = jnp.where(term == degree, product, value)
        return value

    mixed = power(x_pos) * total
    for step, copy in enumerate(copies2):
        copy.wait_recv()
        mixed = mixed + power((x_pos + x_count - step - 1) % x_count) * got2[step]

    pair = jnp.concatenate([mixed, pltpu.roll(mixed, WIN, 1)], axis=0)
    slot0 = jnp.dot(pick0[...], pair, precision=precise, preferred_element_type=jnp.float32)
    slot1 = jnp.dot(pick1[...], pair, precision=precise, preferred_element_type=jnp.float32)
    slot_lane = lax.broadcasted_iota(jnp.int32, (band_count, LOW), 1)
    sent3[...] = jnp.where(slot_lane < WIN, slot0, slot1)
    own = pl.ds(band, 1)
    for peer in peers3:
        pltpu.make_async_remote_copy(
            src_ref=sent3.at[pl.ds(peer, 1), :],
            dst_ref=got3.at[own, :],
            send_sem=send3,
            recv_sem=recv3,
            device_id=(peer, x_pos),
            device_id_type=MESH,
        ).start()
    got3[own, :] = sent3[own, :]

    wide = lax.broadcasted_iota(jnp.int32, (blocks, LOW), 1)
    deep = lax.broadcasted_iota(jnp.int32, (blocks, LOW), 0)
    tile = jnp.zeros((blocks, LOW), jnp.int32)
    for block in range(blocks):
        tile = jnp.where(deep == block, tiles[block], tile)
    clipped = jnp.maximum(tile, 0)
    tile_row = clipped % WIN
    tile_slot = clipped // WIN
    angle = (2.0 * math.pi / WIN) * ((wide % WIN * tile_row) % WIN).astype(jnp.float32)
    angle = jnp.where(wide < WIN, angle, angle - 0.5 * math.pi)
    loads[12].wait()
    sums = jnp.dot(jnp.cos(angle), rows_v[...], precision=precise, preferred_element_type=jnp.float32)
    span = PARTS * z_count
    column = lax.broadcasted_iota(jnp.int32, (blocks, span), 1)
    column_z = column // PARTS
    column_part = column % PARTS
    row_pos = column_z % SIDE * FACET + column_z // SIDE * ROWS + column_part // 2
    slot_v = jnp.where(tile_slot[:, :1] == 0, freq_v[0], freq_v[1])
    angle = (2.0 * math.pi / SKY) * ((slot_v * row_pos) & (SKY - 1)).astype(jnp.float32)
    cosines = jnp.cos(angle)
    sines = jnp.sin(angle)
    real = sums[:, :span] * cosines + sums[:, span:] * sines
    imag = sums[:, span:] * cosines - sums[:, :span] * sines
    usable = tile[:, :1] >= 0
    real = jnp.where(usable, real, 0.0)
    imag = jnp.where(usable, imag, 0.0)
    even = column_part % 2 == 0
    weights[:blocks, :] = jnp.where(even, real, -imag)
    weights[blocks:, :] = jnp.where(even, imag, real)

    everyone = pltpu.make_async_copy(
        sent3.at[: len(peers3), :], got3.at[: len(peers3), :], recv3
    )
    everyone.wait()

    loads[13].wait()
    loads[14].wait()
    lines = jnp.dot(weights[...], got3[...], precision=precise, preferred_element_type=jnp.float32)
    keep = wide // WIN == tile_slot
    lines = jnp.where(jnp.concatenate([keep, keep], axis=0), lines, 0.0)
    spread = jnp.dot(lines, across_v[...], precision=precise, preferred_element_type=jnp.float32)
    crossed = pltpu.roll(spread[blocks:], WIN, 1)
    tile_rows = spread[:blocks] + jnp.where(wide < WIN, -crossed, crossed)
    upright = jnp.transpose(tile_rows)
    for block in range(blocks):
        real_t = upright[:WIN, block : block + 1]
        imag_t = upright[WIN:, block : block + 1]
        real_f = fourier_v[block, :, :LOW]
        imag_f = fourier_v[block, :, LOW:]
        out[block : block + 1, :LOW] = jnp.sum(real_t * real_f - imag_t * imag_f, axis=0, keepdims=True)
        out[block : block + 1, LOW:] = jnp.sum(real_t * imag_f + imag_t * real_f, axis=0, keepdims=True)

    for copy in copies1 + copies2:
        copy.wait_send()
    pltpu.make_async_copy(
        sent3.at[: len(peers3), :], got3.at[: len(peers3), :], send3
    ).wait()


def local(z_count, x_count, taylor, chan_coord, sub_offset, sub_owner, tile_list, fourier):
    constants = tables(z_count, z_count * PARTS)
    half = sub_owner.shape[0] // 2
    blocks = tile_list.shape[0]
    band_count = z_count * PARTS
    outer, twiddle, inner, rows, across = constants
    scratch = [
        pltpu.SMEM(sub_owner.shape, jnp.int32),
        pltpu.SMEM(sub_offset.shape[::-1], jnp.int32),
        pltpu.SMEM(tile_list.shape, jnp.int32),
        pltpu.SMEM(chan_coord.shape, jnp.float32),
        pltpu.VMEM((ROWS, FACET), jnp.float32),
        pltpu.VMEM((blocks, WIN, 2 * LOW), jnp.float32),
        pltpu.VMEM((3 * HIGH, 2 * COARSE), jnp.bfloat16),
        pltpu.VMEM(twiddle.shape, jnp.float32),
        pltpu.VMEM((2 * LOW, 6 * LOW), jnp.bfloat16),
        pltpu.VMEM(rows.shape, jnp.float32),
        pltpu.VMEM(across.shape, jnp.float32),
    ]
    scratch += [
        pltpu.VMEM((ROWS * LOW, 3 * HIGH), jnp.bfloat16),
        pltpu.VMEM((ROWS, LOW, 2 * COARSE), jnp.float32),
        pltpu.VMEM((ROWS, 6 * LOW, COARSE), jnp.bfloat16),
        pltpu.VMEM((COARSE // LOW, PARTS * LOW, LOW), jnp.float32),
        pltpu.VMEM((PARTS * half, LOW), jnp.float32),
        pltpu.VMEM((PARTS - 1, half, LOW), jnp.float32),
        pltpu.VMEM((half, LOW), jnp.float32),
        pltpu.VMEM((max(x_count - 1, 1), half, LOW), jnp.float32),
        pltpu.VMEM((band_count, LOW), jnp.float32),
        pltpu.VMEM((band_count, LOW), jnp.float32),
        pltpu.VMEM((band_count, 2 * half), jnp.float32),
        pltpu.VMEM((band_count, 2 * half), jnp.float32),
        pltpu.VMEM((2 * blocks, band_count), jnp.float32),
        pltpu.SemaphoreType.DMA((15,)),
    ]
    for count in (PARTS, max(x_count, 2)):
        scratch += [pltpu.SemaphoreType.DMA((count - 1,))] * 2
    scratch += [pltpu.SemaphoreType.DMA] * 2
    large = pl.BlockSpec(memory_space=pl.ANY)
    visibilities = pl.pallas_call(
        functools.partial(kernel, z_count, x_count, half),
        out_shape=jax.ShapeDtypeStruct((blocks, 2 * LOW), jnp.float32),
        in_specs=[large] * (6 + len(constants)),
        out_specs=pl.BlockSpec(memory_space=pltpu.VMEM),
        scratch_shapes=scratch,
        compiler_params=pltpu.CompilerParams(collective_id=0, has_side_effects=True),
    )(sub_owner, sub_offset.T, tile_list, chan_coord, taylor, fourier, *[jnp.asarray(table) for table in constants])
    return visibilities[:, None, :]


def solution(mesh):
    return jax.shard_map(
        functools.partial(local, mesh.shape["facet"] // PARTS, mesh.shape["chan"]),
        mesh=mesh,
        in_specs=(
            P("facet", "chan", None, None),
            P(),
            P(),
            P(),
            P("facet"),
            P("facet", "chan", None, None),
        ),
        out_specs=P("facet", "chan", None),
        check_vma=False,
    )
```

time: 45.7 us -> 36 us (0.79)
  Pallas kernels: 42.7 us -> 34.4 us
  local copies, waits for them, and re-layouts: 2.71 us -> 1.34 us
    pallas_call x1, Pallas kernels: 42.7 us -> 34.4 us  [local(): pl.pallas_call(functools.partial(kernel, z_count, x_count, half), out_sha...]
    unnamed x1 -> x0, local copies, waits for them, and re-layouts: 1.37 us -> none
where the time goes in v2:
time: 36 us; the launch traced here: 35.8 us
  Pallas kernels  34.4 us (96%)
  local copies, waits for them, and re-layouts  1.34 us (4%)
    pallas_call x1, Pallas kernels, local(): pl.pallas_call(functools.partial(kernel, z_count, x_count, half), out_sha...  34.4 us
    broadcast_in_dim x1, local copies, waits for them, and re-layouts, local(): return visibilities[:, None, :]  1.34 us

profile of v2, /device:TPU:1, one launch (start us, length us, event | category | flops | bytes accessed | tf_op | source)
XLA Modules:
  0.0 35.8 jit_solution(14657100549426265168)
XLA Ops:
  0.0 34.4 %shard_map.109 = f32[16,256]{1,0:T(8,128)} custom-call(s32[64]{0:T(128)} %owner_h.1, s32[2,64]{1,0:T(2,128)} %bitcast.3, s32[16]{0:T(128)} %tiles_h.1, f32[4]{0:T(128)} %coord_h.1, f32[1,1,4,8192]{3,2,1,0:T(4,128)} %taylor.1, f32[16,1,64,256]{3,2,1,0:T(8,128)} %fourier.1, bf16[2,512,1024]{2,1,0:T(8,128)(2,1)} %constant.10.clone.outer, ...), custom_call_target="tpu_custom_call" | custom-call | tf_op jit(solution)/shard_map/pallas_call | solution.py:424
  34.5 1.3 %copy.12 = f32[16,1,256]{2,1,0:T(1,128)} copy(f32[16,1,256]{2,0,1:T(8,128)} %bitcast.2) | data formatting | bytes 32768 | tf_op jit(solution)/shard_map/broadcast_in_dim | solution.py:432

commit v3 on v2

--- a/solution.py
+++ b/solution.py
@@ -18,6 +18,7 @@
 LOW = 128
 HIGH = FACET // LOW
 COARSE = SKY // LOW
+SPAN = COARSE + LOW
 PARTS = 2 * ROWS
 MESH = pl.DeviceIdType.MESH
 
@@ -41,17 +42,10 @@
     high_pos = np.arange(SIDE * HIGH)
     cosines, sines = turns(high_pos[:, None] * coarse[None, :], COARSE)
     outer = np.stack(halves(np.concatenate([cosines, -sines], axis=1)))
-    cosines, sines = turns(low_pos[:, None] * coarse[None, :], SKY)
+    cosines, sines = turns(low_pos[:, None] * np.arange(SPAN)[None, :], SKY)
     twiddle = np.concatenate([cosines, -sines], axis=1).astype(np.float32)
     cosines, sines = turns(low_pos[:, None] * low_pos[None, :], LOW)
-    full = np.concatenate(
-        [
-            np.concatenate([cosines, sines], axis=1),
-            np.concatenate([-sines, cosines], axis=1),
-        ],
-        axis=0,
-    )
-    inner = np.stack(halves(full))
+    inner = np.concatenate(halves(cosines) + halves(sines), axis=1)
     column = np.arange(PARTS * z_count)
     z_pos = column // PARTS
     row_pos = (z_pos % SIDE) * FACET + (z_pos // SIDE) * ROWS + column % PARTS // 2
@@ -66,14 +60,21 @@
         axis=0,
     )
     cosines, sines = turns(steps[:, None] * steps[None, :], WIN)
-    across = np.concatenate([cosines, sines], axis=1)
-    across = np.concatenate([across] * CAP, axis=0)
+    across = np.concatenate(
+        [
+            np.concatenate([cosines, -sines], axis=1),
+            np.concatenate([sines, cosines], axis=1),
+        ],
+        axis=0,
+    )
+    high, low = halves(across)
+    across = np.concatenate([high, high, low], axis=1)
     return (
         outer,
         twiddle,
         inner,
         rows.astype(np.float32),
-        across.astype(np.float32),
+        across,
     )
 
 
@@ -104,18 +105,20 @@
     inner_v,
     rows_v,
     across_v,
+    offset_v,
+    staged,
     lhs,
+    lines_v,
     coarse_v,
     fine_v,
-    freq,
+    spread_v,
     sent1,
     got1,
     sent2,
     got2,
     sent3,
     got3,
-    pick0,
-    pick1,
+    picks,
     weights,
     load_sem,
     send1,
@@ -141,9 +144,8 @@
             (outer.at[0, pl.ds(pl.multiple_of(part * HIGH, HIGH), HIGH), :], outer_v.at[HIGH : 2 * HIGH, :]),
             (outer.at[1, pl.ds(pl.multiple_of(part * HIGH, HIGH), HIGH), :], outer_v.at[2 * HIGH :, :]),
             (twiddle, twiddle_v),
-            (inner.at[0], inner_v.at[:, : 2 * LOW]),
-            (inner.at[0], inner_v.at[:, 2 * LOW : 4 * LOW]),
-            (inner.at[1], inner_v.at[:, 4 * LOW :]),
+            (offset_h, offset_v),
+            (inner, inner_v),
             (offset_h, offset),
             (owner_h, owner),
             (tiles_h, tiles),
@@ -178,59 +180,79 @@
 
     loads[0].wait()
     for high in range(HIGH):
-        freq[0, pl.ds(high, ROWS, stride=HIGH), :] = taylor_v[:, high * LOW : (high + 1) * LOW]
+        staged[pl.ds(high, ROWS, stride=HIGH), :] = taylor_v[:, high * LOW : (high + 1) * LOW]
     for row in range(ROWS):
-        image = freq[0, row * HIGH : (row + 1) * HIGH, :]
+        image = staged[row * HIGH : (row + 1) * HIGH, :]
         top = image.astype(jnp.bfloat16).astype(jnp.float32)
         stacked = jnp.concatenate([top, image - top, top], axis=0)
         lhs[row * LOW : (row + 1) * LOW, :] = jnp.transpose(stacked).astype(jnp.bfloat16)
 
-    for load in loads[1:8]:
+    loads[5].wait()
+    loads[6].wait()
+    grid_row = lax.broadcasted_iota(jnp.int32, (subs, subs), 0)
+    grid_col = lax.broadcasted_iota(jnp.int32, (subs, subs), 1)
+    diagonal = grid_row == grid_col
+    start = jnp.where(diagonal, offset_v[0:1, :].astype(jnp.float32), 0.0)
+    start = jnp.broadcast_to(jnp.sum(start, axis=1, keepdims=True), (subs, LOW)).astype(jnp.int32)
+    lane = lax.broadcasted_iota(jnp.int32, (subs, LOW), 1)
+    deep = lax.broadcasted_iota(jnp.int32, (subs, LOW), 0)
+    shift = start & (LOW - 1)
+    group_of = (lax.shift_right_logical(start, 7) & 3) + jnp.where(lane < shift, 1, 0)
+    target = (lane + shift + jnp.where(deep >= half, WIN, 0)) & (LOW - 1)
+    chosen = jnp.where(lax.shift_right_logical(start, 9) == lane, 1.0, 0.0).astype(jnp.bfloat16)
+    lines = jnp.dot(chosen, inner_v[...], preferred_element_type=jnp.float32)
+    cos_h, cos_l, sin_h, sin_l = [lines[:, part * LOW : (part + 1) * LOW] for part in range(4)]
+    real_line = jnp.concatenate([cos_h, sin_h, cos_h, sin_h, cos_l, sin_l], axis=1)
+    imag_line = jnp.concatenate([-sin_h, cos_h, -sin_h, cos_h, -sin_l, cos_l], axis=1)
+    lines_v[:subs, :] = real_line.astype(jnp.bfloat16)
+    lines_v[subs:, :] = imag_line.astype(jnp.bfloat16)
+
+    for load in loads[1:5]:
         load.wait()
-    for row in range(ROWS):
+
+    def coarse(row):
         coarse_v[row] = jnp.dot(
             lhs[row * LOW : (row + 1) * LOW, :], outer_v[...], preferred_element_type=jnp.float32
         )
+
+    def turn(row):
         for start in range(0, LOW, 16):
             real_c = coarse_v[row, start : start + 16, :COARSE]
             imag_c = coarse_v[row, start : start + 16, COARSE:]
-            real_t = twiddle_v[start : start + 16, :COARSE]
-            imag_t = twiddle_v[start : start + 16, COARSE:]
+            real_c = jnp.concatenate([real_c, real_c[:, :LOW]], axis=1)
+            imag_c = jnp.concatenate([imag_c, imag_c[:, :LOW]], axis=1)
+            real_t = twiddle_v[start : start + 16, :SPAN]
+            imag_t = twiddle_v[start : start + 16, SPAN:]
             real = real_c * real_t - imag_c * imag_t
             imag = real_c * imag_t + imag_c * real_t
-            for shift, value in ((start, real), (start + LOW, imag)):
+            for place, value in ((start, real), (start + LOW, imag)):
                 top = value.astype(jnp.bfloat16)
                 rest = (value - top.astype(jnp.float32)).astype(jnp.bfloat16)
-                fine_v[row, shift : shift + 16, :] = top
-                fine_v[row, shift + 2 * LOW : shift + 2 * LOW + 16, :] = rest
-                fine_v[row, shift + 4 * LOW : shift + 4 * LOW + 16, :] = top
-        result = jnp.dot(inner_v[...], fine_v[row], preferred_element_type=jnp.float32)
-        for group in range(COARSE // LOW):
-            freq[group, row * 2 * LOW : (row + 1) * 2 * LOW, :] = result[:, group * LOW : (group + 1) * LOW]
-
-    for load in loads[8:12]:
+                fine_v[row, place : place + 16, :] = top
+                fine_v[row, place + 2 * LOW : place + 2 * LOW + 16, :] = rest
+                fine_v[row, place + 4 * LOW : place + 4 * LOW + 16, :] = top
+
+    def fine(row):
+        result = jnp.dot(lines_v[...], fine_v[row], preferred_element_type=jnp.float32)
+        for side in range(2):
+            found = result[side * subs : (side + 1) * subs, :]
+            value = found[:, :LOW]
+            for group in range(1, SPAN // LOW):
+                value = jnp.where(group_of == group, found[:, group * LOW : (group + 1) * LOW], value)
+            value = jnp.take_along_axis(value, target, axis=1, mode="promise_in_bounds")
+            place = (2 * row + side) * half
+            sent1[place : place + half, :] = jnp.where(lane[:half] < WIN, value[:half], value[half:])
+
+    coarse(0)
+    for row in range(ROWS):
+        if row + 1 < ROWS:
+            coarse(row + 1)
+        turn(row)
+        if row:
+            fine(row - 1)
+    fine(ROWS - 1)
+    for load in loads[7:11]:
         load.wait()
-    lane = lax.broadcasted_iota(jnp.int32, (PARTS, LOW), 1)
-    bunch = min(8, half)
-
-    def pick(number, carry):
-        found = []
-        for place in range(bunch):
-            for side in range(2):
-                start = offset[0, number * bunch + place + side * half]
-                shift = start & (LOW - 1)
-                first = lax.shift_right_logical(start, 7)
-                second = (first + 1) & (SKY // LOW - 1)
-                left = freq[first & 3, pl.ds(lax.shift_right_logical(first, 2), PARTS, stride=LOW), :]
-                right = freq[second & 3, pl.ds(lax.shift_right_logical(second, 2), PARTS, stride=LOW), :]
-                value = jnp.where(lane >= shift, left, right)
-                found.append(pltpu.roll(value, (LOW + WIN * side - shift) & (LOW - 1), 1))
-        for place in range(bunch):
-            value = jnp.where(lane < WIN, found[2 * place], found[2 * place + 1])
-            sent1[pl.ds(number * bunch + place, PARTS, stride=half), :] = value
-        return carry
-
-    lax.fori_loop(0, half // bunch, pick, 0)
 
     pl.semaphore_wait(barrier, len(peers_x) + len(greeted))
     copies1 = []
@@ -259,19 +281,19 @@
         freq_v[0] = jnp.where(own & (seen == 0), offset[1, sub], freq_v[0])
         freq_v[1] = jnp.where(own & (seen == 1), offset[1, sub], freq_v[1])
         seen = seen + own.astype(jnp.int32)
-    grid_row = lax.broadcasted_iota(jnp.int32, (subs, subs), 0)
-    grid_col = lax.broadcasted_iota(jnp.int32, (subs, subs), 1)
     plain_f = plain[:1].astype(jnp.float32)
     swapped_f = swapped[:1].astype(jnp.float32)
-    along = jnp.sum(jnp.where(grid_row == grid_col, plain_f, 0.0), axis=1, keepdims=True)
+    along = jnp.sum(jnp.where(diagonal, plain_f, 0.0), axis=1, keepdims=True)
     place = lax.broadcasted_iota(jnp.int32, (band_count, subs), 0).astype(jnp.float32)
-    for target, holders, number, wanted in (
-        (pick0, plain_f, grid_col, 0.0),
-        (pick1, swapped_f, (grid_col + half) % subs, 1.0),
+    for holders, number, wanted in (
+        (plain_f, grid_col, 0.0),
+        (swapped_f, (grid_col + half) % subs, 1.0),
     ):
         same = jnp.where((along == holders) & (grid_row < number), 1.0, 0.0)
         rank = jnp.sum(same, axis=0, keepdims=True)
-        target[...] = jnp.where((place == holders) & (rank == wanted), 1.0, 0.0)
+        value = jnp.where((place == holders) & (rank == wanted), 1.0, 0.0)
+        first = 2 * subs * int(wanted)
+        picks[:, first : first + 2 * subs] = jnp.concatenate([value, value], axis=1).astype(jnp.bfloat16)
 
     total = sent1[pl.ds(pl.multiple_of(part * half, half), half), :]
     for step, copy in enumerate(copies1):
@@ -307,10 +329,11 @@
         mixed = mixed + power((x_pos + x_count - step - 1) % x_count) * got2[step]
 
     pair = jnp.concatenate([mixed, pltpu.roll(mixed, WIN, 1)], axis=0)
-    slot0 = jnp.dot(pick0[...], pair, precision=precise, preferred_element_type=jnp.float32)
-    slot1 = jnp.dot(pick1[...], pair, precision=precise, preferred_element_type=jnp.float32)
-    slot_lane = lax.broadcasted_iota(jnp.int32, (band_count, LOW), 1)
-    sent3[...] = jnp.where(slot_lane < WIN, slot0, slot1)
+    top = pair.astype(jnp.bfloat16).astype(jnp.float32)
+    terms = jnp.concatenate([top, pair - top], axis=0)
+    side = lax.broadcasted_iota(jnp.int32, (2 * subs, LOW), 1) < WIN
+    terms = jnp.concatenate([jnp.where(side, terms, 0.0), jnp.where(side, 0.0, terms)], axis=0)
+    sent3[...] = jnp.dot(picks[...], terms.astype(jnp.bfloat16), preferred_element_type=jnp.float32)
     own = pl.ds(band, 1)
     for peer in peers3:
         pltpu.make_async_remote_copy(
@@ -333,7 +356,7 @@
     tile_slot = clipped // WIN
     angle = (2.0 * math.pi / WIN) * ((wide % WIN * tile_row) % WIN).astype(jnp.float32)
     angle = jnp.where(wide < WIN, angle, angle - 0.5 * math.pi)
-    loads[12].wait()
+    loads[11].wait()
     sums = jnp.dot(jnp.cos(angle), rows_v[...], precision=precise, preferred_element_type=jnp.float32)
     span = PARTS * z_count
     column = lax.broadcasted_iota(jnp.int32, (blocks, span), 1)
@@ -350,28 +373,47 @@
     real = jnp.where(usable, real, 0.0)
     imag = jnp.where(usable, imag, 0.0)
     even = column_part % 2 == 0
-    weights[:blocks, :] = jnp.where(even, real, -imag)
-    weights[blocks:, :] = jnp.where(even, imag, real)
+    for first, value in ((0, jnp.where(even, real, -imag)), (blocks, jnp.where(even, imag, real))):
+        top = value.astype(jnp.bfloat16)
+        rest = (value - top.astype(jnp.float32)).astype(jnp.bfloat16)
+        weights[first : first + blocks, :span] = top
+        weights[first : first + blocks, span : 2 * span] = top
+        weights[first : first + blocks, 2 * span :] = rest
+
+    loads[12].wait()
+    loads[13].wait()
+    for block in range(0, blocks, 2):
+        value = jnp.concatenate(
+            [
+                jnp.concatenate([fourier_v[block, :, :LOW], fourier_v[block, :, LOW:]], axis=0),
+                jnp.concatenate([fourier_v[block + 1, :, :LOW], fourier_v[block + 1, :, LOW:]], axis=0),
+            ],
+            axis=1,
+        )
+        top = value.astype(jnp.bfloat16)
+        rest = (value - top.astype(jnp.float32)).astype(jnp.bfloat16)
+        stacked = jnp.concatenate([top, rest, top], axis=0)
+        spread_v[block // 2] = jnp.dot(across_v[...], stacked, preferred_element_type=jnp.float32)
 
     everyone = pltpu.make_async_copy(
         sent3.at[: len(peers3), :], got3.at[: len(peers3), :], recv3
     )
     everyone.wait()
 
-    loads[13].wait()
-    loads[14].wait()
-    lines = jnp.dot(weights[...], got3[...], precision=precise, preferred_element_type=jnp.float32)
-    keep = wide // WIN == tile_slot
-    lines = jnp.where(jnp.concatenate([keep, keep], axis=0), lines, 0.0)
-    spread = jnp.dot(lines, across_v[...], precision=precise, preferred_element_type=jnp.float32)
-    crossed = pltpu.roll(spread[blocks:], WIN, 1)
-    tile_rows = spread[:blocks] + jnp.where(wide < WIN, -crossed, crossed)
-    upright = jnp.transpose(tile_rows)
+    value = got3[...]
+    top = value.astype(jnp.bfloat16)
+    rest = (value - top.astype(jnp.float32)).astype(jnp.bfloat16)
+    stacked = jnp.concatenate([top, rest, top], axis=0)
+    lines = jnp.dot(weights[...], stacked, preferred_element_type=jnp.float32)
+    first_slot = jnp.concatenate([tile_slot, tile_slot], axis=0) == 0
+    lines = jnp.where(first_slot, lines, pltpu.roll(lines, WIN, 1))
+    upright = jnp.transpose(lines)
     for block in range(blocks):
         real_t = upright[:WIN, block : block + 1]
-        imag_t = upright[WIN:, block : block + 1]
-        real_f = fourier_v[block, :, :LOW]
-        imag_f = fourier_v[block, :, LOW:]
+        imag_t = upright[:WIN, blocks + block : blocks + block + 1]
+        place = block % 2 * LOW
+        real_f = spread_v[block // 2, :WIN, place : place + LOW]
+        imag_f = spread_v[block // 2, WIN:, place : place + LOW]
         out[block : block + 1, :LOW] = jnp.sum(real_t * real_f - imag_t * imag_f, axis=0, keepdims=True)
         out[block : block + 1, LOW:] = jnp.sum(real_t * imag_f + imag_t * real_f, axis=0, keepdims=True)
 
@@ -397,25 +439,27 @@
         pltpu.VMEM((blocks, WIN, 2 * LOW), jnp.float32),
         pltpu.VMEM((3 * HIGH, 2 * COARSE), jnp.bfloat16),
         pltpu.VMEM(twiddle.shape, jnp.float32),
-        pltpu.VMEM((2 * LOW, 6 * LOW), jnp.bfloat16),
+        pltpu.VMEM(inner.shape, jnp.bfloat16),
         pltpu.VMEM(rows.shape, jnp.float32),
-        pltpu.VMEM(across.shape, jnp.float32),
+        pltpu.VMEM(across.shape, jnp.bfloat16),
+        pltpu.VMEM(sub_offset.shape[::-1], jnp.int32),
+        pltpu.VMEM((ROWS * HIGH, LOW), jnp.float32),
     ]
     scratch += [
         pltpu.VMEM((ROWS * LOW, 3 * HIGH), jnp.bfloat16),
+        pltpu.VMEM((4 * half, 6 * LOW), jnp.bfloat16),
         pltpu.VMEM((ROWS, LOW, 2 * COARSE), jnp.float32),
-        pltpu.VMEM((ROWS, 6 * LOW, COARSE), jnp.bfloat16),
-        pltpu.VMEM((COARSE // LOW, PARTS * LOW, LOW), jnp.float32),
+        pltpu.VMEM((ROWS, 6 * LOW, SPAN), jnp.bfloat16),
+        pltpu.VMEM((blocks // 2, 2 * WIN, 2 * LOW), jnp.float32),
         pltpu.VMEM((PARTS * half, LOW), jnp.float32),
         pltpu.VMEM((PARTS - 1, half, LOW), jnp.float32),
         pltpu.VMEM((half, LOW), jnp.float32),
         pltpu.VMEM((max(x_count - 1, 1), half, LOW), jnp.float32),
         pltpu.VMEM((band_count, LOW), jnp.float32),
         pltpu.VMEM((band_count, LOW), jnp.float32),
-        pltpu.VMEM((band_count, 2 * half), jnp.float32),
-        pltpu.VMEM((band_count, 2 * half), jnp.float32),
-        pltpu.VMEM((2 * blocks, band_count), jnp.float32),
-        pltpu.SemaphoreType.DMA((15,)),
+        pltpu.VMEM((band_count, 8 * half), jnp.bfloat16),
+        pltpu.VMEM((2 * blocks, 3 * band_count), jnp.bfloat16),
+        pltpu.SemaphoreType.DMA((14,)),
     ]
     for count in (PARTS, max(x_count, 2)):
         scratch += [pltpu.SemaphoreType.DMA((count - 1,))] * 2

time: 36 us -> 35.4 us (0.983)
  Pallas kernels: 34.4 us -> 33.8 us
    pallas_call x1, Pallas kernels: 34.4 us -> 33.8 us  [local(): pl.pallas_call(functools.partial(kernel, z_count, x_count, half), out_sha...]
where the time goes in v3:
time: 35.4 us; the launch traced here: 35.2 us
  Pallas kernels  33.8 us (95%)
  local copies, waits for them, and re-layouts  1.34 us (4%)
    pallas_call x1, Pallas kernels, local(): pl.pallas_call(functools.partial(kernel, z_count, x_count, half), out_sha...  33.8 us
    broadcast_in_dim x1, local copies, waits for them, and re-layouts, local(): return visibilities[:, None, :]  1.34 us

profile of v3, /device:TPU:1, one launch (start us, length us, event | category | flops | bytes accessed | tf_op | source)
XLA Modules:
  0.0 35.2 jit_solution(18117854575743011115)
XLA Ops:
  0.0 33.8 %shard_map.109 = f32[16,256]{1,0:T(8,128)} custom-call(s32[64]{0:T(128)} %owner_h.1, s32[2,64]{1,0:T(2,128)} %bitcast.3, s32[16]{0:T(128)} %tiles_h.1, f32[4]{0:T(128)} %coord_h.1, f32[1,1,4,8192]{3,2,1,0:T(4,128)} %taylor.1, f32[16,1,64,256]{3,2,1,0:T(8,128)} %fourier.1, bf16[2,512,1024]{2,1,0:T(8,128)(2,1)} %constant.10.clone.outer, ...), custom_call_target="tpu_custom_call" | custom-call | tf_op jit(solution)/shard_map/pallas_call | solution.py:468
  33.8 1.3 %copy.12 = f32[16,1,256]{2,1,0:T(1,128)} copy(f32[16,1,256]{2,0,1:T(8,128)} %bitcast.2) | data formatting | bytes 32768 | tf_op jit(solution)/shard_map/broadcast_in_dim | solution.py:476

commit v4 on v3

--- a/solution.py
+++ b/solution.py
@@ -471,8 +471,11 @@
         in_specs=[large] * (6 + len(constants)),
         out_specs=pl.BlockSpec(memory_space=pltpu.VMEM),
         scratch_shapes=scratch,
-        compiler_params=pltpu.CompilerParams(collective_id=0, has_side_effects=True),
-    )(sub_owner, sub_offset.T, tile_list, chan_coord, taylor, fourier, *[jnp.asarray(table) for table in constants])
+        compiler_params=pltpu.CompilerParams(collective_id=0, has_side_effects=True, vmem_limit_bytes=26 * 2**20),
+    )(*[
+        pltpu.with_memory_space_constraint(value, pltpu.HBM)
+        for value in (sub_owner, sub_offset.T, tile_list, chan_coord, taylor, fourier, *[jnp.asarray(table) for table in constants])
+    ])
     return visibilities[:, None, :]
 
 

time: 35.4 us -> 34 us (0.960)
  local copies, waits for them, and re-layouts: 1.34 us -> 0.62 us
  Pallas kernels: 33.8 us -> 33.2 us
    broadcast_in_dim x1, local copies, waits for them, and re-layouts: 1.34 us -> 0.62 us  [local(): return visibilities[:, None, :]]
    pallas_call x1, Pallas kernels: 33.8 us -> 33.2 us  [local(): pl.pallas_call(functools.partial(kernel, z_count, x_count, half), out_sha...]
where the time goes in v4:
time: 34 us; the launch traced here: 33.9 us
  Pallas kernels  33.2 us (98%)
  local copies, waits for them, and re-layouts  0.62 us (2%)
    pallas_call x1, Pallas kernels, local(): pl.pallas_call(functools.partial(kernel, z_count, x_count, half), out_sha...  33.2 us

profile of v4, /device:TPU:1, one launch (start us, length us, event | category | flops | bytes accessed | tf_op | source)
XLA Modules:
  0.0 33.9 jit_solution(4766451544766832727)
XLA Ops:
  0.0 33.2 %shard_map.109 = f32[16,256]{1,0:T(8,128)S(1)} custom-call(s32[64]{0:T(128)} %owner_h.1, s32[2,64]{1,0:T(2,128)} %bitcast.3, s32[16]{0:T(128)} %tiles_h.1, f32[4]{0:T(128)} %coord_h.1, f32[1,1,4,8192]{3,2,1,0:T(4,128)} %taylor.1, f32[16,1,64,256]{3,2,1,0:T(8,128)} %fourier.1, bf16[2,512,1024]{2,1,0:T(8,128)(2,1)} %constant.10.clone.outer, ...), custom_call_target="tpu_custom_call" | custom-call | tf_op jit(solution)/shard_map/pallas_call | solution.py:468
  33.2 0.6 %copy.12 = f32[16,1,256]{2,1,0:T(1,128)} copy(f32[16,1,256]{2,0,1:T(8,128)S(1)} %bitcast.2) | data formatting | bytes 32768 | tf_op jit(solution)/shard_map/broadcast_in_dim | solution.py:479

commit v5 on v4

--- a/solution.py
+++ b/solution.py
@@ -42,7 +42,8 @@
     high_pos = np.arange(SIDE * HIGH)
     cosines, sines = turns(high_pos[:, None] * coarse[None, :], COARSE)
     outer = np.stack(halves(np.concatenate([cosines, -sines], axis=1)))
-    cosines, sines = turns(low_pos[:, None] * np.arange(SPAN)[None, :], SKY)
+    rows = np.concatenate([16 * np.arange(LOW // 16), np.arange(16)])
+    cosines, sines = turns(rows[:, None] * np.arange(SPAN)[None, :], SKY)
     twiddle = np.concatenate([cosines, -sines], axis=1).astype(np.float32)
     cosines, sines = turns(low_pos[:, None] * low_pos[None, :], LOW)
     inner = np.concatenate(halves(cosines) + halves(sines), axis=1)
@@ -101,6 +102,7 @@
     taylor_v,
     fourier_v,
     outer_v,
+    small_v,
     twiddle_v,
     inner_v,
     rows_v,
@@ -140,11 +142,10 @@
     for number, (source, target) in enumerate(
         [
             (taylor.at[0, 0], taylor_v),
+            (offset_h, offset_v),
+            (twiddle, small_v),
             (outer.at[0, pl.ds(pl.multiple_of(part * HIGH, HIGH), HIGH), :], outer_v.at[:HIGH, :]),
-            (outer.at[0, pl.ds(pl.multiple_of(part * HIGH, HIGH), HIGH), :], outer_v.at[HIGH : 2 * HIGH, :]),
-            (outer.at[1, pl.ds(pl.multiple_of(part * HIGH, HIGH), HIGH), :], outer_v.at[2 * HIGH :, :]),
-            (twiddle, twiddle_v),
-            (offset_h, offset_v),
+            (outer.at[1, pl.ds(pl.multiple_of(part * HIGH, HIGH), HIGH), :], outer_v.at[HIGH:, :]),
             (inner, inner_v),
             (offset_h, offset),
             (owner_h, owner),
@@ -165,9 +166,11 @@
 
     barrier = pltpu.get_barrier_semaphore()
     far = sorted(range(z_count), key=lambda step: -min(step, z_count - step))
-    peers_x = [wrapped(x_pos, step, x_count) for step in range(1, x_count)]
+    steps_x = sorted(range(1, x_count), key=lambda step: -min(step, x_count - step))
+    steps1 = sorted(range(1, PARTS), key=lambda step: -min(step, PARTS - step))
+    peers_x = [wrapped(x_pos, step, x_count) for step in steps_x]
     parts = [wrapped(part, step, PARTS) for step in range(PARTS)]
-    peers1 = [z_pos * PARTS + peer for peer in parts[1:]]
+    peers1 = [z_pos * PARTS + parts[step] for step in steps1]
     peers3 = []
     for step in far:
         base = wrapped(z_pos, step, z_count) * PARTS
@@ -178,6 +181,17 @@
     for peer in peers_x:
         pl.semaphore_signal(barrier, inc=1, device_id=(band, peer), device_id_type=MESH)
 
+    loads[2].wait()
+    for high in range(LOW // 16):
+        for first in range(0, SPAN, LOW):
+            real_h = small_v[high : high + 1, first : first + LOW]
+            imag_h = small_v[high : high + 1, SPAN + first : SPAN + first + LOW]
+            real_l = small_v[LOW // 16 :, first : first + LOW]
+            imag_l = small_v[LOW // 16 :, SPAN + first : SPAN + first + LOW]
+            place = slice(high * 16, high * 16 + 16)
+            twiddle_v[place, first : first + LOW] = real_h * real_l - imag_h * imag_l
+            twiddle_v[place, SPAN + first : SPAN + first + LOW] = real_h * imag_l + imag_h * real_l
+
     loads[0].wait()
     for high in range(HIGH):
         staged[pl.ds(high, ROWS, stride=HIGH), :] = taylor_v[:, high * LOW : (high + 1) * LOW]
@@ -187,8 +201,8 @@
         stacked = jnp.concatenate([top, image - top, top], axis=0)
         lhs[row * LOW : (row + 1) * LOW, :] = jnp.transpose(stacked).astype(jnp.bfloat16)
 
+    loads[1].wait()
     loads[5].wait()
-    loads[6].wait()
     grid_row = lax.broadcasted_iota(jnp.int32, (subs, subs), 0)
     grid_col = lax.broadcasted_iota(jnp.int32, (subs, subs), 1)
     diagonal = grid_row == grid_col
@@ -207,12 +221,14 @@
     lines_v[:subs, :] = real_line.astype(jnp.bfloat16)
     lines_v[subs:, :] = imag_line.astype(jnp.bfloat16)
 
-    for load in loads[1:5]:
-        load.wait()
+    loads[3].wait()
+    loads[4].wait()
 
     def coarse(row):
+        top = outer_v[:HIGH, :]
+        table = jnp.concatenate([top, top, outer_v[HIGH:, :]], axis=0)
         coarse_v[row] = jnp.dot(
-            lhs[row * LOW : (row + 1) * LOW, :], outer_v[...], preferred_element_type=jnp.float32
+            lhs[row * LOW : (row + 1) * LOW, :], table, preferred_element_type=jnp.float32
         )
 
     def turn(row):
@@ -230,10 +246,10 @@
                 rest = (value - top.astype(jnp.float32)).astype(jnp.bfloat16)
                 fine_v[row, place : place + 16, :] = top
                 fine_v[row, place + 2 * LOW : place + 2 * LOW + 16, :] = rest
-                fine_v[row, place + 4 * LOW : place + 4 * LOW + 16, :] = top
 
     def fine(row):
-        result = jnp.dot(lines_v[...], fine_v[row], preferred_element_type=jnp.float32)
+        data = jnp.concatenate([fine_v[row], fine_v[row, : 2 * LOW, :]], axis=0)
+        result = jnp.dot(lines_v[...], data, preferred_element_type=jnp.float32)
         for side in range(2):
             found = result[side * subs : (side + 1) * subs, :]
             value = found[:, :LOW]
@@ -251,14 +267,14 @@
         if row:
             fine(row - 1)
     fine(ROWS - 1)
-    for load in loads[7:11]:
+    for load in loads[6:10]:
         load.wait()
 
     pl.semaphore_wait(barrier, len(peers_x) + len(greeted))
     copies1 = []
     for step, peer in enumerate(peers1):
         copy = pltpu.make_async_remote_copy(
-            src_ref=sent1.at[pl.ds(pl.multiple_of(parts[step + 1] * half, half), half), :],
+            src_ref=sent1.at[pl.ds(pl.multiple_of(parts[steps1[step]] * half, half), half), :],
             dst_ref=got1.at[step],
             send_sem=send1.at[step],
             recv_sem=recv1.at[step],
@@ -326,7 +342,7 @@
     mixed = power(x_pos) * total
     for step, copy in enumerate(copies2):
         copy.wait_recv()
-        mixed = mixed + power((x_pos + x_count - step - 1) % x_count) * got2[step]
+        mixed = mixed + power((x_pos + x_count - steps_x[step]) % x_count) * got2[step]
 
     pair = jnp.concatenate([mixed, pltpu.roll(mixed, WIN, 1)], axis=0)
     top = pair.astype(jnp.bfloat16).astype(jnp.float32)
@@ -356,7 +372,7 @@
     tile_slot = clipped // WIN
     angle = (2.0 * math.pi / WIN) * ((wide % WIN * tile_row) % WIN).astype(jnp.float32)
     angle = jnp.where(wide < WIN, angle, angle - 0.5 * math.pi)
-    loads[11].wait()
+    loads[10].wait()
     sums = jnp.dot(jnp.cos(angle), rows_v[...], precision=precise, preferred_element_type=jnp.float32)
     span = PARTS * z_count
     column = lax.broadcasted_iota(jnp.int32, (blocks, span), 1)
@@ -380,8 +396,8 @@
         weights[first : first + blocks, span : 2 * span] = top
         weights[first : first + blocks, 2 * span :] = rest
 
+    loads[11].wait()
     loads[12].wait()
-    loads[13].wait()
     for block in range(0, blocks, 2):
         value = jnp.concatenate(
             [
@@ -393,7 +409,21 @@
         top = value.astype(jnp.bfloat16)
         rest = (value - top.astype(jnp.float32)).astype(jnp.bfloat16)
         stacked = jnp.concatenate([top, rest, top], axis=0)
-        spread_v[block // 2] = jnp.dot(across_v[...], stacked, preferred_element_type=jnp.float32)
+        spread = jnp.dot(across_v[...], stacked, preferred_element_type=jnp.float32)
+        for side in range(2):
+            real_f = spread[:WIN, side * LOW : (side + 1) * LOW]
+            imag_f = spread[WIN:, side * LOW : (side + 1) * LOW]
+            value = jnp.concatenate(
+                [
+                    jnp.concatenate([real_f, imag_f], axis=1),
+                    jnp.concatenate([-imag_f, real_f], axis=1),
+                ],
+                axis=0,
+            )
+            top = value.astype(jnp.bfloat16)
+            place = (block + side) * LOW
+            spread_v[0, place : place + LOW, :] = top
+            spread_v[1, place : place + LOW, :] = (value - top.astype(jnp.float32)).astype(jnp.bfloat16)
 
     everyone = pltpu.make_async_copy(
         sent3.at[: len(peers3), :], got3.at[: len(peers3), :], recv3
@@ -407,15 +437,15 @@
     lines = jnp.dot(weights[...], stacked, preferred_element_type=jnp.float32)
     first_slot = jnp.concatenate([tile_slot, tile_slot], axis=0) == 0
     lines = jnp.where(first_slot, lines, pltpu.roll(lines, WIN, 1))
-    upright = jnp.transpose(lines)
-    for block in range(blocks):
-        real_t = upright[:WIN, block : block + 1]
-        imag_t = upright[:WIN, blocks + block : blocks + block + 1]
-        place = block % 2 * LOW
-        real_f = spread_v[block // 2, :WIN, place : place + LOW]
-        imag_f = spread_v[block // 2, WIN:, place : place + LOW]
-        out[block : block + 1, :LOW] = jnp.sum(real_t * real_f - imag_t * imag_f, axis=0, keepdims=True)
-        out[block : block + 1, LOW:] = jnp.sum(real_t * imag_f + imag_t * real_f, axis=0, keepdims=True)
+    value = jnp.where(wide < WIN, lines[:blocks], pltpu.roll(lines[blocks:], WIN, 1))
+    top = value.astype(jnp.bfloat16).astype(jnp.float32)
+    stacked = jnp.concatenate([top, value - top], axis=0)
+    deep = lax.broadcasted_iota(jnp.int32, (2 * blocks, LOW), 0) % blocks
+    spread = jnp.concatenate([jnp.where(deep == block, stacked, 0.0) for block in range(blocks)], axis=1)
+    spread = spread.astype(jnp.bfloat16)
+    result = jnp.dot(spread, spread_v[0], preferred_element_type=jnp.float32)
+    rest = jnp.dot(spread[:blocks], spread_v[1], preferred_element_type=jnp.float32)
+    out[...] = result[:blocks] + result[blocks:] + rest
 
     for copy in copies1 + copies2:
         copy.wait_send()
@@ -437,8 +467,9 @@
         pltpu.SMEM(chan_coord.shape, jnp.float32),
         pltpu.VMEM((ROWS, FACET), jnp.float32),
         pltpu.VMEM((blocks, WIN, 2 * LOW), jnp.float32),
-        pltpu.VMEM((3 * HIGH, 2 * COARSE), jnp.bfloat16),
+        pltpu.VMEM((2 * HIGH, 2 * COARSE), jnp.bfloat16),
         pltpu.VMEM(twiddle.shape, jnp.float32),
+        pltpu.VMEM((LOW, 2 * SPAN), jnp.float32),
         pltpu.VMEM(inner.shape, jnp.bfloat16),
         pltpu.VMEM(rows.shape, jnp.float32),
         pltpu.VMEM(across.shape, jnp.bfloat16),
@@ -449,8 +480,8 @@
         pltpu.VMEM((ROWS * LOW, 3 * HIGH), jnp.bfloat16),
         pltpu.VMEM((4 * half, 6 * LOW), jnp.bfloat16),
         pltpu.VMEM((ROWS, LOW, 2 * COARSE), jnp.float32),
-        pltpu.VMEM((ROWS, 6 * LOW, SPAN), jnp.bfloat16),
-        pltpu.VMEM((blocks // 2, 2 * WIN, 2 * LOW), jnp.float32),
+        pltpu.VMEM((ROWS, 4 * LOW, SPAN), jnp.bfloat16),
+        pltpu.VMEM((2, blocks * LOW, 2 * LOW), jnp.bfloat16),
         pltpu.VMEM((PARTS * half, LOW), jnp.float32),
         pltpu.VMEM((PARTS - 1, half, LOW), jnp.float32),
         pltpu.VMEM((half, LOW), jnp.float32),
@@ -459,7 +490,7 @@
         pltpu.VMEM((band_count, LOW), jnp.float32),
         pltpu.VMEM((band_count, 8 * half), jnp.bfloat16),
         pltpu.VMEM((2 * blocks, 3 * band_count), jnp.bfloat16),
-        pltpu.SemaphoreType.DMA((14,)),
+        pltpu.SemaphoreType.DMA((13,)),
     ]
     for count in (PARTS, max(x_count, 2)):
         scratch += [pltpu.SemaphoreType.DMA((count - 1,))] * 2

time: 34 us -> 33.9 us (level)
  no operation moved by 1% of the time
where the time goes in v5:
time: 33.9 us; the launch traced here: 33.8 us
  Pallas kernels  33.2 us (98%)
  local copies, waits for them, and re-layouts  0.62 us (2%)
    pallas_call x1, Pallas kernels, local(): pl.pallas_call(functools.partial(kernel, z_count, x_count, half), out_sha...  33.2 us

profile of v5, /device:TPU:1, one launch (start us, length us, event | category | flops | bytes accessed | tf_op | source)
XLA Modules:
  0.0 33.8 jit_solution(1636984818675528320)
XLA Ops:
  0.0 33.2 %shard_map.109 = f32[16,256]{1,0:T(8,128)S(1)} custom-call(s32[64]{0:T(128)} %owner_h.1, s32[2,64]{1,0:T(2,128)} %bitcast.3, s32[16]{0:T(128)} %tiles_h.1, f32[4]{0:T(128)} %coord_h.1, f32[1,1,4,8192]{3,2,1,0:T(4,128)} %taylor.1, f32[16,1,64,256]{3,2,1,0:T(8,128)} %fourier.1, bf16[2,512,1024]{2,1,0:T(8,128)(2,1)} %constant.10.clone.outer, ...), custom_call_target="tpu_custom_call" | custom-call | tf_op jit(solution)/shard_map/pallas_call | solution.py:499
  33.2 0.6 %copy.12 = f32[16,1,256]{2,1,0:T(1,128)} copy(f32[16,1,256]{2,0,1:T(8,128)S(1)} %bitcast.2) | data formatting | bytes 32768 | tf_op jit(solution)/shard_map/broadcast_in_dim | solution.py:510
